TPU v7x, 32 devices: a whole 2x2x4 slice. The times are simulated.
32 devices in a mesh: dp: 2 (over y), ctx: 4 (over z), fsdp: 4 (over x, core).
Axes of the slice: x: 2, y: 2, z: 4, core: 2. Of those that a mesh axis runs over, the one named last changes fastest.
Arguments:
- layer_input: bfloat16 [8, 2048, 768], P(('dp', 'fsdp'), 'ctx'), may hold values from -6 to 6
- first_values: bfloat16 [8, 2048, 384], P(('dp', 'fsdp'), 'ctx'), may hold values from -6 to 6
- segment_ids: int32 [8, 2048], P(('dp', 'fsdp')), may hold values from 0 to 7, never falling along the last dimension, each value on 1 to 1024 neighbouring positions
- pairing: int32 [8], replicated, may hold values from 0 to 7, as said below
- norm_gains: bfloat16 [2, 768], P(None, 'fsdp'), may hold values from 0.099609375 to 1.8984375
- norm_biases: bfloat16 [2, 768], P(None, 'fsdp'), may hold values from -2 to 2
- w_qkv: bfloat16 [768, 1920], P('fsdp'), may hold values from -0.21875 to 0.21875
- w_out: bfloat16 [768, 768], P('fsdp'), may hold values from -0.875 to 0.875
- w_up: bfloat16 [768, 3072], P(None, 'fsdp'), may hold values from -0.21875 to 0.21875
- w_down: bfloat16 [3072, 768], P('fsdp'), may hold values from -0.109375 to 0.109375
- cotangent: bfloat16 [8, 2048, 768], P(('dp', 'fsdp'), 'ctx'), may hold values from -6 to 6
Outputs:
- layer_out: bfloat16 [8, 2048, 768], P(('dp', 'fsdp'), 'ctx')
- input_grad: float32 [8, 2048, 768], P(('dp', 'fsdp'), 'ctx')
- first_values_grad: float32 [8, 2048, 384], P(('dp', 'fsdp'), 'ctx')
- gains_grad: float32 [2, 768], P(None, 'fsdp')
- biases_grad: float32 [2, 768], P(None, 'fsdp')
- qkv_grad: float32 [768, 1920], P('fsdp')
- out_grad: float32 [768, 768], P('fsdp')
- up_grad: float32 [768, 3072], P(None, 'fsdp')
- down_grad: float32 [3072, 768], P('fsdp')
Inputs may be any that keep to these rules, and one draw needn't show every extreme that they name: `segment_ids`: along each sequence the ids never fall; each document holds 1 to 1024 positions, one exactly that many. `pairing`: every block is named once; entries 2c and 2c + 1 name blocks b and 7 - b for some b, in either order.
All inputs are finite; a program needn't handle non-finite values.
Results may differ from a plain program's by a relative error of at most 0.019.
Values may be sent and summed in bfloat16 or wider, within the bound.
No kernel may reach another device: no remote copies, remote signals or barrier semaphores. Data moves between devices by JAX's collectives and lax.ppermute only.
A program may use at most 192 MiB of HBM per device.

v0:
```python
import jax
import jax.numpy as jnp
from jax import lax
from jax.sharding import PartitionSpec as P

D = 768
HEADS = 12
HD = 64
VH = 6


EPSILON = 1e-05
NEGATIVE = -1e30


def norm_layer(values_in, gain, bias):
    center = jnp.mean(values_in, axis=-1, keepdims=True)
    centred = values_in - center
    spread = jnp.mean(centred * centred, axis=-1, keepdims=True)
    return centred * lax.rsqrt(spread + EPSILON) * gain + bias


def gelu_tanh(values_in):
    return jax.nn.gelu(values_in, approximate=True)


def block_scores(query_part, key_part, query_pos, query_doc, key_pos, key_doc):
    scale = HD ** (-0.5)
    raw = (
        jnp.einsum("rhd,khd->hrk", query_part, key_part, preferred_element_type=jnp.float32) * scale
    )
    allowed = (key_pos[None, :] <= query_pos[:, None]) & (key_doc[None, :] == query_doc[:, None])
    return (raw, allowed[None])


def body(
    layer_input,
    first_values,
    segment_ids,
    pairing,
    norm_gains,
    norm_biases,
    w_qkv,
    w_out,
    w_up,
    w_down,
    cotangent,
):
    scale = HD ** (-0.5)
    ctx_index = lax.axis_index("ctx")
    local_rows = layer_input.shape[1]
    half_rows = local_rows // 2
    seq_length = local_rows * lax.axis_size("ctx")
    key_block = min(512, seq_length)
    key_count = seq_length // key_block
    offsets = jnp.arange(half_rows, dtype=jnp.int32)
    all_pos = (pairing[:, None] * half_rows + offsets[None, :]).reshape(seq_length)
    own_blocks = lax.dynamic_slice_in_dim(pairing, 2 * ctx_index, 2)
    own_pos = (own_blocks[:, None] * half_rows + offsets[None, :]).reshape(local_rows)
    doc_row = segment_ids[0]
    all_doc = jnp.take(doc_row, all_pos)
    own_doc = jnp.take(doc_row, own_pos)
    gathered = (
        lax.all_gather(norm_gains, "fsdp", axis=1, tiled=True),
        lax.all_gather(norm_biases, "fsdp", axis=1, tiled=True),
        lax.all_gather(w_qkv, "fsdp", axis=0, tiled=True),
        lax.all_gather(w_out, "fsdp", axis=0, tiled=True),
        lax.all_gather(w_up, "fsdp", axis=1, tiled=True),
        lax.all_gather(w_down, "fsdp", axis=0, tiled=True),
    )
    gains_all, biases_all, qkv_full, out_full, up_full, down_full = gathered
    gains = gains_all.astype(jnp.float32)
    biases = biases_all.astype(jnp.float32)
    inputs = layer_input[0].astype(jnp.float32)
    normed_one, norm_one_back = jax.vjp(norm_layer, inputs, gains[0], biases[0])
    h_one = normed_one.astype(jnp.bfloat16)
    qkv_low = jnp.dot(h_one, qkv_full, preferred_element_type=jnp.float32).astype(jnp.bfloat16)
    query_low = qkv_low[:, :D]
    key_low = qkv_low[:, D : 2 * D]
    fresh_low = qkv_low[:, 2 * D :]
    values_low = jnp.concatenate([fresh_low, first_values[0]], axis=1)
    keys_all, values_all = (
        lax.all_gather(key_low, "ctx", axis=0, tiled=True),
        lax.all_gather(values_low, "ctx", axis=0, tiled=True),
    )
    query_heads = query_low.reshape(local_rows, HEADS, HD)
    key_blocks = keys_all.reshape(key_count, key_block, HEADS, HD)
    value_blocks = values_all.reshape(key_count, key_block, HEADS, HD)
    pos_blocks = all_pos.reshape(key_count, key_block)
    doc_blocks = all_doc.reshape(key_count, key_block)

    def stats_step(carry, block):
        running_top, running_total = carry
        key_part, key_pos, key_doc = block
        raw, allowed = block_scores(query_heads, key_part, own_pos, own_doc, key_pos, key_doc)
        masked = jnp.where(allowed, raw, NEGATIVE)
        new_top = jnp.maximum(running_top, jnp.max(masked, axis=-1))
        terms = jnp.where(allowed, jnp.exp(raw - new_top[..., None]), 0.0)
        running_total = running_total * jnp.exp(running_top - new_top) + jnp.sum(terms, axis=-1)
        return ((new_top, running_total), None)

    start_top = jnp.full((HEADS, local_rows), NEGATIVE, jnp.float32)
    start_total = jnp.zeros((HEADS, local_rows), jnp.float32)
    (final_top, final_total), _ = lax.scan(
        stats_step, (start_top, start_total), (key_blocks, pos_blocks, doc_blocks)
    )
    log_total = final_top + jnp.log(final_total)

    def mix_step(accum, block):
        key_part, value_part, key_pos, key_doc = block
        raw, allowed = block_scores(query_heads, key_part, own_pos, own_doc, key_pos, key_doc)
        probs = jnp.where(allowed, jnp.exp(raw - log_total[..., None]), 0.0).astype(jnp.bfloat16)
        return (
            accum
            + jnp.einsum("hrk,khd->rhd", probs, value_part, preferred_element_type=jnp.float32),
            None,
        )

    mixed, _ = lax.scan(
        mix_step,
        jnp.zeros((local_rows, HEADS, HD), jnp.float32),
        (key_blocks, value_blocks, pos_blocks, doc_blocks),
    )
    attn_low = mixed.reshape(local_rows, D).astype(jnp.bfloat16)
    resid = inputs + jnp.dot(attn_low, out_full, preferred_element_type=jnp.float32)
    normed_two, norm_two_back = jax.vjp(norm_layer, resid, gains[1], biases[1])
    h_two = normed_two.astype(jnp.bfloat16)
    upper = jnp.dot(h_two, up_full, preferred_element_type=jnp.float32)
    active, gelu_back = jax.vjp(gelu_tanh, upper)
    active_low = active.astype(jnp.bfloat16)
    layer_out = (resid + jnp.dot(active_low, down_full, preferred_element_type=jnp.float32)).astype(
        jnp.bfloat16
    )
    regathered = (
        lax.all_gather(norm_gains, "fsdp", axis=1, tiled=True),
        lax.all_gather(norm_biases, "fsdp", axis=1, tiled=True),
        lax.all_gather(w_qkv, "fsdp", axis=0, tiled=True),
        lax.all_gather(w_out, "fsdp", axis=0, tiled=True),
        lax.all_gather(w_up, "fsdp", axis=1, tiled=True),
        lax.all_gather(w_down, "fsdp", axis=0, tiled=True),
    )
    qkv_back = regathered[2]
    out_back = regathered[3]
    up_back = regathered[4]
    down_back = regathered[5]
    cot_low = cotangent[0]
    cot_full = cot_low.astype(jnp.float32)
    down_grad = jnp.dot(active_low.T, cot_low, preferred_element_type=jnp.float32)
    dactive = jnp.dot(cot_low, down_back.T, preferred_element_type=jnp.float32)
    dupper_low = gelu_back(dactive)[0].astype(jnp.bfloat16)
    up_grad = jnp.dot(h_two.T, dupper_low, preferred_element_type=jnp.float32)
    dh_two = jnp.dot(dupper_low, up_back.T, preferred_element_type=jnp.float32)
    dresid_norm, gain_two_grad, bias_two_grad = norm_two_back(dh_two)
    dresid = cot_full + dresid_norm
    dbranch_low = dresid.astype(jnp.bfloat16)
    out_grad = jnp.dot(attn_low.T, dbranch_low, preferred_element_type=jnp.float32)
    dmixed_low = jnp.dot(dbranch_low, out_back.T, preferred_element_type=jnp.float32).astype(
        jnp.bfloat16
    )
    dmixed_heads = dmixed_low.reshape(local_rows, HEADS, HD)
    row_terms = jnp.sum(dmixed_heads.astype(jnp.float32) * mixed, axis=-1).T

    def grad_step(accum, block):
        key_part, value_part, key_pos, key_doc = block
        raw, allowed = block_scores(query_heads, key_part, own_pos, own_doc, key_pos, key_doc)
        probs = jnp.where(allowed, jnp.exp(raw - log_total[..., None]), 0.0)
        dprobs = jnp.einsum(
            "rhd,khd->hrk", dmixed_heads, value_part, preferred_element_type=jnp.float32
        )
        dscore_low = (probs * (dprobs - row_terms[..., None])).astype(jnp.bfloat16)
        accum = accum + jnp.einsum(
            "hrk,khd->rhd", dscore_low, key_part, preferred_element_type=jnp.float32
        )
        dkey_part = jnp.einsum(
            "hrk,rhd->khd", dscore_low, query_heads, preferred_element_type=jnp.float32
        )
        dvalue_part = jnp.einsum(
            "hrk,rhd->khd",
            probs.astype(jnp.bfloat16),
            dmixed_heads,
            preferred_element_type=jnp.float32,
        )
        return (accum, (dkey_part, dvalue_part))

    dquery_sum, (dkey_parts, dvalue_parts) = lax.scan(
        grad_step,
        jnp.zeros((local_rows, HEADS, HD), jnp.float32),
        (key_blocks, value_blocks, pos_blocks, doc_blocks),
    )
    dkeys_all = dkey_parts.reshape(seq_length, D) * scale
    dvalues_all = dvalue_parts.reshape(seq_length, D)
    own_dkeys, own_dvalues = (
        lax.psum_scatter(
            dkeys_all.astype(jnp.bfloat16), "ctx", scatter_dimension=0, tiled=True
        ).astype(jnp.float32),
        lax.psum_scatter(
            dvalues_all.astype(jnp.bfloat16), "ctx", scatter_dimension=0, tiled=True
        ).astype(jnp.float32),
    )
    dquery = dquery_sum.reshape(local_rows, D) * scale
    fresh_width = VH * HD
    first_grad = own_dvalues[:, fresh_width:]
    dqkv_low = jnp.concatenate(
        [
            dquery.astype(jnp.bfloat16),
            own_dkeys.astype(jnp.bfloat16),
            own_dvalues[:, :fresh_width].astype(jnp.bfloat16),
        ],
        axis=1,
    )
    qkv_grad = jnp.dot(h_one.T, dqkv_low, preferred_element_type=jnp.float32)
    dh_one = jnp.dot(dqkv_low, qkv_back.T, preferred_element_type=jnp.float32)
    dinput_norm, gain_one_grad, bias_one_grad = norm_one_back(dh_one)
    input_grad = dresid + dinput_norm
    gain_grads = jnp.stack([gain_one_grad, gain_two_grad])
    bias_grads = jnp.stack([bias_one_grad, bias_two_grad])
    shares = (
        lax.psum_scatter(
            gain_grads.astype(jnp.bfloat16), "fsdp", scatter_dimension=1, tiled=True
        ).astype(jnp.float32),
        lax.psum_scatter(
            bias_grads.astype(jnp.bfloat16), "fsdp", scatter_dimension=1, tiled=True
        ).astype(jnp.float32),
        lax.psum_scatter(
            qkv_grad.astype(jnp.bfloat16), "fsdp", scatter_dimension=0, tiled=True
        ).astype(jnp.float32),
        lax.psum_scatter(
            out_grad.astype(jnp.bfloat16), "fsdp", scatter_dimension=0, tiled=True
        ).astype(jnp.float32),
        lax.psum_scatter(
            up_grad.astype(jnp.bfloat16), "fsdp", scatter_dimension=1, tiled=True
        ).astype(jnp.float32),
        lax.psum_scatter(
            down_grad.astype(jnp.bfloat16), "fsdp", scatter_dimension=0, tiled=True
        ).astype(jnp.float32),
    )
    summed = (
        lax.psum(shares[0].astype(jnp.bfloat16), ("dp", "ctx")).astype(jnp.float32),
        lax.psum(shares[1].astype(jnp.bfloat16), ("dp", "ctx")).astype(jnp.float32),
        lax.psum(shares[2].astype(jnp.bfloat16), ("dp", "ctx")).astype(jnp.float32),
        lax.psum(shares[3].astype(jnp.bfloat16), ("dp", "ctx")).astype(jnp.float32),
        lax.psum(shares[4].astype(jnp.bfloat16), ("dp", "ctx")).astype(jnp.float32),
        lax.psum(shares[5].astype(jnp.bfloat16), ("dp", "ctx")).astype(jnp.float32),
    )
    return (
        layer_out[None],
        input_grad[None],
        first_grad[None],
        summed[0],
        summed[1],
        summed[2],
        summed[3],
        summed[4],
        summed[5],
    )


def solution(mesh):
    in_specs = (
        P(("dp", "fsdp"), "ctx", None),
        P(("dp", "fsdp"), "ctx", None),
        P(("dp", "fsdp"), None),
        P(),
        P(None, "fsdp"),
        P(None, "fsdp"),
        P("fsdp", None),
        P("fsdp", None),
        P(None, "fsdp"),
        P("fsdp", None),
        P(("dp", "fsdp"), "ctx", None),
    )
    out_specs = (
        P(("dp", "fsdp"), "ctx", None),
        P(("dp", "fsdp"), "ctx", None),
        P(("dp", "fsdp"), "ctx", None),
        P(None, "fsdp"),
        P(None, "fsdp"),
        P("fsdp", None),
        P("fsdp", None),
        P(None, "fsdp"),
        P("fsdp", None),
    )
    return jax.shard_map(body, mesh=mesh, in_specs=in_specs, out_specs=out_specs, check_vma=False)
```

profile of v0, /device:TPU:0, one launch (start us, length us, event | category | flops | bytes accessed | tf_op | source)
XLA Modules:
  0.0 874.5 jit_solution(13623779563315954214)
XLA Ops:
  8.0 6.3 all-gather
  14.3 5.5 all-gather.1
  23.6 16.1 %all-gather.9.cloned.1.call-done = bf16[768,1920]{1,0:T(8,128)(2,1)} async-done(((bf16[192,1920]{1,0:T(8,128)(2,1)}), bf16[768,1920]{1,0:T(8,128)(2,1)}) %all-gather.9.cloned.1.call-update) | async-done | bytes 2949136 | tf_op jit(solution)/shard_map/all_gather | solution.py:66
  51.7 11.8 %gather_fusion = s32[2048]{0:T(1024)S(1)} fusion(s32[2048]{0:T(1024)S(1)} %bitcast.284, s32[2048]{0:T(1024)S(1)} %broadcast_clamp_fusion), kind=kCustom, calls=%fused_computation | custom fusion | bytes 24576 | tf_op jit(solution)/shard_map/jit(_take)/gather | solution.py:61
  65.0 43.7 %all-gather.13.cloned.1.call-done = bf16[2048,768]{1,0:T(8,128)(2,1)} async-done(((bf16[512,768]{1,0:T(8,128)(2,1)}), bf16[2048,768]{1,0:T(8,128)(2,1)}) %all-gather.13.cloned.1.call-update) | async-done | bytes 3145744 | tf_op jit(solution)/shard_map/all_gather | solution.py:83
  113.4 6.3 reshape.387
  123.9 24.9 %while.39 = (s32[]{:T(128)}, f32[12,512]{1,0:T(8,128)S(1)}, f32[12,512]{1,0:T(8,128)S(1)}, s32[4,512]{1,0:T(4,128)S(1)}, s32[4,512]{1,0:T(4,128)S(1)}, /*index=5...) while((s32[]{:T(128)}, f32[12,512]{1,0:T(8,128)S(1)}, ...), condition=%wide.region_5.6_spmd.clone, body=%wide.region_2.5_spmd.clone.sunk | while | flops 425490944 | bytes 27867280 | solution.py:104
  148.8 24.2 %all-gather.11.cloned.1.call-done = bf16[2048,768]{1,0:T(8,128)(2,1)} async-done(((bf16[512,768]{1,0:T(8,128)(2,1)}), bf16[2048,768]{1,0:T(8,128)(2,1)}) %all-gather.11.cloned.1.call-update) | async-done | bytes 3145744 | tf_op jit(solution)/shard_map/all_gather | solution.py:84
  177.7 6.2 reshape.386
  188.3 23.0 %while.40 = (s32[]{:T(128)}, f32[512,12,64]{0,2,1:T(8,128)S(1)}, bf16[4,512,12,64]{1,3,2,0:T(8,128)(2,1)}, s32[4,512]{1,0:T(4,128)S(1)}, s32[4,512]{1,0:T(4,128)...) while((s32[]{:T(128)}, f32[512,12,64]{0,2,1:T(8,128)S(1)}, ...), condition=%wide.region_7.8_spmd.clone, body=%wide.region_6.7_spmd.clone.sunk | while | flops 819462656 | bytes 6078098 | solution.py:119
  216.2 13.3 %all-gather.17.cloned.1.call-done = bf16[768,3072]{1,0:T(8,128)(2,1)} async-done(((bf16[768,768]{1,0:T(8,128)(2,1)}), bf16[768,3072]{1,0:T(8,128)(2,1)}) %all-gather.17.cloned.1.call-update) | async-done | bytes 4718608 | tf_op jit(solution)/shard_map/all_gather | solution.py:68
  229.5 8.2 fusion.88
  237.7 30.7 %all-gather.19.cloned.1.call-done = bf16[3072,768]{1,0:T(8,128)(2,1)} async-done(((bf16[768,768]{1,0:T(8,128)(2,1)}), bf16[3072,768]{1,0:T(8,128)(2,1)}) %all-gather.19.cloned.1.call-update) | async-done | bytes 4718608 | tf_op jit(solution)/shard_map/all_gather | solution.py:69
  268.4 9.3 %fusion.58 = bf16[512,3072]{1,0:T(8,128)(2,1)S(1)} fusion(f32[512,3072]{1,0:T(8,128)} %fusion.88, bf16[3072,768]{1,0:T(8,128)(2,1)} %all-gather.19.cloned.1.call-done, bf16[1,512,768]{2,1,0:T(8,128)(2,1)S(1)} %copy-done.13), kind=kOutput, calls=%fused_computation.72 | convolution fusion | flops 2447376384 | bytes 14942208 | tf_op jit(solution)/shard_map/dot_general | solution.py:149
  287.0 88.2 %while.41 = (s32[]{:T(128)}, f32[512,12,64]{0,2,1:T(8,128)}, f32[4,512,12,64]{1,3,2,0:T(8,128)}, bf16[4,512,12,64]{1,3,2,0:T(8,128)(2,1)}, bf16[4,512,12,64]{1,3...) while((s32[]{:T(128)}, f32[512,12,64]{0,2,1:T(8,128)}, ...), condition=%wide.region_14.15_spmd.clone, body=%wide.region_13.14_spmd.clone.sunk | while | flops 2046296576 | bytes 81885488 | solution.py:185
  296.2 5.8 fusion.154
  317.8 5.8 fusion.154
  340.0 5.8 fusion.154
  362.2 5.8 fusion.154
  394.5 6.5 convolution_convert_fusion.1
  402.1 8.3 convolution_convert_fusion
  412.9 29.8 %reduce-scatter.15.cloned.1.call-done = bf16[512,768]{0,1:T(8,128)(2,1)} async-done(((bf16[2048,768]{0,1:T(8,128)(2,1)}), bf16[512,768]{0,1:T(8,128)(2,1)}) %reduce-scatter.15.cloned.1.call-update) | async-done | bytes 786448 | tf_op jit(solution)/shard_map/reduce_scatter | solution.py:196
  444.9 60.4 %reduce-scatter.13.cloned.1.call-done = bf16[512,768]{0,1:T(8,128)(2,1)} async-done(((bf16[2048,768]{0,1:T(8,128)(2,1)}), bf16[512,768]{0,1:T(8,128)(2,1)}) %reduce-scatter.13.cloned.1.call-update) | async-done | bytes 786448 | tf_op jit(solution)/shard_map/reduce_scatter | solution.py:193
  518.9 15.4 %reduce-scatter.19.cloned.1.call-done = bf16[192,768]{1,0:T(8,128)(2,1)} async-done(((bf16[768,768]{1,0:T(8,128)(2,1)}), bf16[192,768]{1,0:T(8,128)(2,1)}) %reduce-scatter.19.cloned.1.call-update) | async-done | bytes 294928 | tf_op jit(solution)/shard_map/reduce_scatter | solution.py:227
  534.2 50.4 %reduce-scatter.21.cloned.1.call-done = bf16[768,768]{1,0:T(8,128)(2,1)} async-done(((bf16[768,3072]{1,0:T(8,128)(2,1)}), bf16[768,768]{1,0:T(8,128)(2,1)}) %reduce-scatter.21.cloned.1.call-update) | async-done | bytes 1179664 | tf_op jit(solution)/shard_map/reduce_scatter | solution.py:230
  584.7 50.4 %reduce-scatter.23.cloned.1.call-done = bf16[768,768]{1,0:T(8,128)(2,1)} async-done(((bf16[3072,768]{1,0:T(8,128)(2,1)}), bf16[768,768]{1,0:T(8,128)(2,1)}) %reduce-scatter.23.cloned.1.call-update) | async-done | bytes 1179664 | tf_op jit(solution)/shard_map/reduce_scatter | solution.py:233
  635.1 39.3 %reduce-scatter.17.cloned.1.call-done = bf16[192,1920]{1,0:T(8,128)(2,1)} async-done(((bf16[768,1920]{1,0:T(8,128)(2,1)}), bf16[192,1920]{1,0:T(8,128)(2,1)}) %reduce-scatter.17.cloned.1.call-update) | async-done | bytes 737296 | tf_op jit(solution)/shard_map/reduce_scatter | solution.py:224
  674.4 9.3 %fusion.72 = bf16[1,512,768]{2,1,0:T(8,128)(2,1)} fusion(f32[512,768]{1,0:T(8,128)} %copy-done.9, bf16[3072,768]{1,0:T(8,128)(2,1)} %all-gather.19.cloned.1.call-done, f32[512,3072]{1,0:T(8,128)} %fusion.88), kind=kOutput, calls=%fused_computation.108 | convolution fusion | flops 2430861312 | bytes 13369344 | tf_op jit(solution)/shard_map/dot_general | solution.py:131
  689.3 7.8 reduce-scatter.25.cloned.1.call-done
  698.1 21.2 %reduce-scatter.27.cloned.1.call-done = bf16[192,2]{1,0:T(8,128)(2,1)} async-done(((bf16[768,2]{1,0:T(8,128)(2,1)}), bf16[192,2]{1,0:T(8,128)(2,1)}) %reduce-scatter.27.cloned.1.call-update) | async-done | bytes 784
  720.1 22.1 %all-reduce = (bf16[2,192]{1,0:T(2,128)(2,1)S(1)}, bf16[2,192]{1,0:T(2,128)(2,1)S(1)}) all-reduce(bf16[2,192]{1,0:T(2,128)(2,1)S(1)} %copy.92, bf16[2,192]{1,0:T(2,128)(2,1)S(1)} %copy.94), channel_id=1, replica_groups=mesh['dp'=2,'ctx'=4,'fsdp'=4] {'dp','ctx'}, use_global_device_ids=true, to_apply=%region_22.23 | all-reduce | flops 768 | bytes 3072 | tf_op jit(solution)/shard_map/psum | solution.py:238
  743.4 116.9 %all-reduce.4.cloned.1.call-done = (bf16[192,1920]{1,0:T(8,128)(2,1)}, bf16[192,768]{1,0:T(8,128)(2,1)}, bf16[768,768]{1,0:T(8,128)(2,1)}, bf16[768,768]{1,0:T(8,128)(2,1)}) async-done(((bf16[192,1920]{1,0:T(8,128)(2,1)}, bf16[192,768]{1,0:T(8,128)(2,1)}, bf16[768,768]{1,0:T(8,128)(2,1)}, bf16[768,768]{1,0:T(8,128)(2,1)}), (bf16[192,1920]{1,0:T(8,128)(2,1)}, bf16[192,768]{1,0:T(8,128)(2,1)}, ...) | async-done | bytes 3391504 | tf_op jit(solution)/shard_map/psum | solution.py:240
  (312 shorter events, 216.4 us)
Async XLA Ops:
  7.2 41.4 %copy-start = (s32[1,2048]{1,0:T(1,128)S(1)}, s32[1,2048]{1,0:T(1,128)}, u32[]{:S(2)}) copy-start(s32[1,2048]{1,0:T(1,128)} %param.19) | copy-start | bytes 24580
  7.2 32.5 %all-gather.9.cloned.1.call-start = ((), (), s32[]{:S(2)}) async-start(), calls=%async_computation.8 | async-start | bytes 3686400 | tf_op jit(solution)/shard_map/all_gather | solution.py:66
  7.9 100.7 %all-gather.13.cloned.1.call-start = ((), (), s32[]{:S(2)}) async-start(), calls=%async_computation.10 | async-start | bytes 3932160 | tf_op jit(solution)/shard_map/all_gather | solution.py:83
  20.0 19.8 %copy-start.24 = (f32[768]{0:T(1024)}, f32[768]{0:T(1024)S(1)}, u32[]{:S(2)}) copy-start(f32[768]{0:T(1024)S(1)} %get-tuple-element.570) | copy-start | bytes 9220
  20.0 19.8 %copy-start.34 = (f32[768]{0:T(1024)}, f32[768]{0:T(1024)S(1)}, u32[]{:S(2)}) copy-start(f32[768]{0:T(1024)S(1)} %get-tuple-element.475) | copy-start | bytes 9220
  21.5 18.2 %copy-start.26 = (f32[512]{0:T(512)}, f32[512]{0:T(512)S(1)}, u32[]{:S(2)}) copy-start(f32[512]{0:T(512)S(1)} %broadcast_multiply_fusion.1) | copy-start | bytes 6148
  23.6 16.2 %copy-start.28 = (f32[512]{0:T(512)}, f32[512]{0:T(512)S(1)}, u32[]{:S(2)}) copy-start(f32[512]{0:T(512)S(1)} %fusion.81) | copy-start | bytes 6148
  45.0 128.0 %all-gather.11.cloned.1.call-start = ((), (), s32[]{:S(2)}) async-start(), calls=%async_computation.9 | async-start | bytes 3932160 | tf_op jit(solution)/shard_map/all_gather | solution.py:84
  46.1 166.2 %all-gather.15.cloned.1.call-start = ((), (), s32[]{:S(2)}) async-start(), calls=%async_computation.11 | async-start | bytes 1474560 | tf_op jit(solution)/shard_map/all_gather | solution.py:67
  46.7 182.8 %all-gather.17.cloned.1.call-start = ((), (), s32[]{:S(2)}) async-start(), calls=%async_computation.12 | async-start | bytes 5898240 | tf_op jit(solution)/shard_map/all_gather | solution.py:68
  47.3 221.1 %all-gather.19.cloned.1.call-start = ((), (), s32[]{:S(2)}) async-start(), calls=%async_computation.13 | async-start | bytes 5898240 | tf_op jit(solution)/shard_map/all_gather | solution.py:69
  47.8 394.9 %reduce-scatter.15.cloned.1.call-start = ((), (), s32[]{:S(2)}) async-start(), calls=%async_computation.15 | async-start | bytes 3932160 | tf_op jit(solution)/shard_map/reduce_scatter | solution.py:196
  188.3 24.0 %copy-start.7 = (bf16[1,512,768]{2,1,0:T(8,128)(2,1)S(1)}, bf16[1,512,768]{2,1,0:T(8,128)(2,1)}, u32[]{:S(2)}) copy-start(bf16[1,512,768]{2,1,0:T(8,128)(2,1)} %param.17) | copy-start | bytes 2359300
  229.5 38.9 %copy-start.13 = (bf16[1,512,768]{2,1,0:T(8,128)(2,1)S(1)}, bf16[1,512,768]{2,1,0:T(8,128)(2,1)}, u32[]{:S(2)}) copy-start(bf16[1,512,768]{2,1,0:T(8,128)(2,1)} %param.27) | copy-start | bytes 2359300
  268.4 9.3 %copy-start.10 = (f32[512,768]{1,0:T(8,128)S(1)}, f32[512,768]{1,0:T(8,128)}, u32[]{:S(2)}) copy-start(f32[512,768]{1,0:T(8,128)} %copy-done.9) | copy-start | bytes 4718596
  268.4 9.3 %copy-start.36 = (bf16[768,3072]{1,0:T(8,128)(2,1)S(1)}, bf16[768,3072]{1,0:T(8,128)(2,1)}, u32[]{:S(2)}) copy-start(bf16[768,3072]{1,0:T(8,128)(2,1)} %all-gather.17.cloned.1.call-done) | copy-start | bytes 14155780
  382.3 123.0 %reduce-scatter.13.cloned.1.call-start = ((), (), s32[]{:S(2)}) async-start(), calls=%async_computation.14 | async-start | bytes 3932160 | tf_op jit(solution)/shard_map/reduce_scatter | solution.py:193
  391.3 143.0 %reduce-scatter.19.cloned.1.call-start = ((), (), s32[]{:S(2)}) async-start(), calls=%async_computation.17 | async-start | bytes 1474560 | tf_op jit(solution)/shard_map/reduce_scatter | solution.py:227
  394.4 190.2 %reduce-scatter.21.cloned.1.call-start = ((), (), s32[]{:S(2)}) async-start(), calls=%async_computation.18 | async-start | bytes 5898240 | tf_op jit(solution)/shard_map/reduce_scatter | solution.py:230
  401.0 234.0 %reduce-scatter.23.cloned.1.call-start = ((), (), s32[]{:S(2)}) async-start(), calls=%async_computation.19 | async-start | bytes 5898240 | tf_op jit(solution)/shard_map/reduce_scatter | solution.py:233
  410.4 94.9 %copy-start.8 = (bf16[1,512,768]{2,1,0:T(8,128)(2,1)S(1)}, bf16[1,512,768]{2,1,0:T(8,128)(2,1)}, u32[]{:S(2)}) copy-start(bf16[1,512,768]{2,1,0:T(8,128)(2,1)} %param.17) | copy-start | bytes 2359300
  410.5 94.9 %copy-start.25 = (f32[768]{0:T(1024)S(1)}, f32[768]{0:T(1024)}, u32[]{:S(2)}) copy-start(f32[768]{0:T(1024)} %copy-done.24) | copy-start | bytes 9220
  410.5 94.9 %copy-start.27 = (f32[512]{0:T(512)S(1)}, f32[512]{0:T(512)}, u32[]{:S(2)}) copy-start(f32[512]{0:T(512)} %copy-done.26) | copy-start | bytes 6148
  410.5 94.8 %copy-start.29 = (f32[512]{0:T(512)S(1)}, f32[512]{0:T(512)}, u32[]{:S(2)}) copy-start(f32[512]{0:T(512)} %copy-done.28) | copy-start | bytes 6148
  410.5 94.8 %copy-start.35 = (f32[768]{0:T(1024)S(1)}, f32[768]{0:T(1024)}, u32[]{:S(2)}) copy-start(f32[768]{0:T(1024)} %copy-done.34) | copy-start | bytes 9220
  410.5 263.9 %reduce-scatter.17.cloned.1.call-start = ((), (), s32[]{:S(2)}) async-start(), calls=%async_computation.16 | async-start | bytes 3686400 | tf_op jit(solution)/shard_map/reduce_scatter | solution.py:224
  510.5 186.6 %reduce-scatter.25.cloned.1.call-start = ((), (), s32[]{:S(2)}) async-start(), calls=%async_computation.20 | async-start | bytes 245760
  517.6 201.6 %reduce-scatter.27.cloned.1.call-start = ((), (), s32[]{:S(2)}) async-start(), calls=%async_computation.21 | async-start | bytes 245760
  518.6 341.7 %all-reduce.4.cloned.1.call-start = ((), (), s32[]{:S(2)}) async-start(), calls=%async_computation.22 | async-start | bytes 6782976 | tf_op jit(solution)/shard_map/psum | solution.py:240
  674.4 11.7 %copy-start.6 = (f32[512,768]{1,0:T(8,128)S(1)}, f32[512,768]{1,0:T(8,128)}, u32[]{:S(2)}) copy-start(f32[512,768]{1,0:T(8,128)} %copy-done.5) | copy-start | bytes 4718596
  674.4 11.7 %copy-start.31 = (f32[512]{0:T(512)S(1)}, f32[512]{0:T(512)}, u32[]{:S(2)}) copy-start(f32[512]{0:T(512)} %copy-done.30) | copy-start | bytes 6148
  860.3 5.9 copy-start.17
  (35 other events, 80.6 us)
Sparse Core Ops, SparseCore 0:
  9.6 30.1 all-gather.8
  45.1 63.4 all-gather.12
  110.8 62.1 all-gather.10
  174.4 16.0 all-gather.14
  192.0 37.4 all-gather.16
  230.9 37.4 all-gather.18
  382.4 60.2 reduce-scatter.14
  445.0 60.2 reduce-scatter.12
  508.5 25.7 reduce-scatter.18
  536.8 47.8 reduce-scatter.20
  587.2 47.8 reduce-scatter.22
  637.6 36.7 reduce-scatter.16
  677.4 19.7 reduce-scatter.24
  699.5 19.7 reduce-scatter.26
  723.1 137.1 all-reduce.3
where the time goes:
time: 879 us; the launch traced here: 875 us
  waiting for transfers between devices  522 us (59%)
  matrix products  180 us (20%)
  local copies, waits for them, and re-layouts  80.6 us (9%)
  other arithmetic  41 us (5%)
  blocking collectives  33.8 us (4%)
  between operations  14.8 us (2%)
    psum x1, waiting for transfers between devices, body(): lax.psum(shares[2].astype(jnp.bfloat16), ('dp', 'ctx')).astype(jnp.float32)  117 us
    reduce_scatter x1, waiting for transfers between devices, body(): lax.psum_scatter(dkeys_all.astype(jnp.bfloat16), 'ctx', scatter_dimension...  60.4 us
    reduce_scatter x1, waiting for transfers between devices, body(): lax.psum_scatter(up_grad.astype(jnp.bfloat16), 'fsdp', scatter_dimension=...  50.4 us
    reduce_scatter x1, waiting for transfers between devices, body(): lax.psum_scatter(down_grad.astype(jnp.bfloat16), 'fsdp', scatter_dimensio...  50.4 us
    all_gather x1, waiting for transfers between devices, body(): lax.all_gather(key_low, 'ctx', axis=0, tiled=True)  43.7 us
    reduce_scatter x1, waiting for transfers between devices, body(): lax.psum_scatter(qkv_grad.astype(jnp.bfloat16), 'fsdp', scatter_dimension...  39.3 us
    unnamed x17, waiting for transfers between devices  31.5 us
    all_gather x1, waiting for transfers between devices, body(): lax.all_gather(w_down, 'fsdp', axis=0, tiled=True)  30.7 us
  transfers between devices with their start and end apart: 15, of which 14 were waited for; matrix products, arithmetic and copies ran while one was open for 19% of the time, Pallas kernels for 0%

commit v1 on v0

--- a/solution.py
+++ b/solution.py
@@ -1,6 +1,10 @@
+import functools
+
 import jax
 import jax.numpy as jnp
 from jax import lax
+from jax.experimental import pallas as pl
+from jax.experimental.pallas import tpu as pltpu
 from jax.sharding import PartitionSpec as P
 
 D = 768
@@ -33,7 +37,7 @@
     return (raw, allowed[None])
 
 
-def body(
+def wide_body(
     layer_input,
     first_values,
     segment_ids,
@@ -255,7 +259,490 @@
     )
 
 
+BLK = 256
+GW = 3 * HD
+LOG2E = 1.4426950408889634
+
+
+def block_rows(index):
+    return pl.ds(pl.multiple_of(index, BLK), BLK)
+
+
+def attn_fwd_kernel(roff, jmin, start_ref, qkv_ref, o_ref, ot_ref, lse_ref, vt_ref, m_ref, l_ref, acc_ref):
+    blocks = qkv_ref.shape[0] // BLK
+    factor = HD ** (-0.5) * LOG2E
+    iota_k = lax.broadcasted_iota(jnp.int32, (BLK, BLK), 0)
+    iota_q = lax.broadcasted_iota(jnp.int32, (BLK, BLK), 1)
+
+    def flip(p, carry):
+        rows = block_rows(roff[p])
+        for h in range(3):
+            vt_ref[h, p] = qkv_ref[rows, 2 * GW + h * HD : 2 * GW + (h + 1) * HD].T
+        return carry
+
+    lax.fori_loop(0, blocks, flip, 0)
+
+    def query_block(i, carry):
+        rows = block_rows(roff[i])
+        start = start_ref[pl.ds(i, 1), :]
+        qts = [qkv_ref[rows, h * HD : (h + 1) * HD].T for h in range(3)]
+        for h in range(3):
+            m_ref[h] = jnp.full((1, BLK), NEGATIVE, jnp.float32)
+            l_ref[h] = jnp.zeros((1, BLK), jnp.float32)
+            acc_ref[h] = jnp.zeros((HD, BLK), jnp.float32)
+
+        def step(j, causal):
+            krows = block_rows(roff[j])
+            allowed = iota_k + j * BLK >= start
+            if causal:
+                allowed = allowed & (iota_k <= iota_q)
+            for h in range(3):
+                kh = qkv_ref[krows, GW + h * HD : GW + (h + 1) * HD]
+                st = jnp.dot(kh, qts[h], preferred_element_type=jnp.float32) * factor
+                st = jnp.where(allowed, st, NEGATIVE)
+                m_old = m_ref[h]
+                m_new = jnp.maximum(m_old, jnp.max(st, axis=0, keepdims=True))
+                pt = jnp.exp2(st - m_new)
+                alpha = jnp.exp2(m_old - m_new)
+                m_ref[h] = m_new
+                l_ref[h] = l_ref[h] * alpha + jnp.sum(pt, axis=0, keepdims=True)
+                acc_ref[h] = acc_ref[h] * alpha + jnp.dot(
+                    vt_ref[h, j], pt.astype(jnp.bfloat16), preferred_element_type=jnp.float32
+                )
+
+        def off_diagonal(j, c):
+            step(j, False)
+            return c
+
+        lax.fori_loop(jmin[i], i, off_diagonal, 0)
+        step(i, True)
+        for h in range(3):
+            total = l_ref[h]
+            ot = acc_ref[h] / total
+            ot_ref[h, i] = ot
+            lse_ref[h, pl.ds(i, 1), :] = m_ref[h] + jnp.log2(total)
+            o_ref[rows, h * HD : (h + 1) * HD] = ot.T.astype(jnp.bfloat16)
+        return carry
+
+    lax.fori_loop(0, blocks, query_block, 0)
+
+
+def attn_bwd_kernel(roff, jmin, start_ref, qkv_ref, do_ref, ot_ref, lse_ref, out_ref, kt_ref, dqt_ref, dk_ref, dv_ref):
+    blocks = qkv_ref.shape[0] // BLK
+    scale = HD ** (-0.5)
+    factor = scale * LOG2E
+    iota_k = lax.broadcasted_iota(jnp.int32, (BLK, BLK), 0)
+    iota_q = lax.broadcasted_iota(jnp.int32, (BLK, BLK), 1)
+
+    def prepare(p, carry):
+        rows = block_rows(roff[p])
+        for h in range(3):
+            kt_ref[h, p] = qkv_ref[rows, GW + h * HD : GW + (h + 1) * HD].T
+            dk_ref[h, p] = jnp.zeros((BLK, HD), jnp.float32)
+            dv_ref[h, p] = jnp.zeros((BLK, HD), jnp.float32)
+        return carry
+
+    lax.fori_loop(0, blocks, prepare, 0)
+
+    def query_block(i, carry):
+        rows = block_rows(roff[i])
+        start = start_ref[pl.ds(i, 1), :]
+        qs = [qkv_ref[rows, h * HD : (h + 1) * HD] for h in range(3)]
+        qts = [q.T for q in qs]
+        dos = [do_ref[rows, h * HD : (h + 1) * HD] for h in range(3)]
+        dots = [d.T for d in dos]
+        lses = [lse_ref[h, pl.ds(i, 1), :] for h in range(3)]
+        deltas = [
+            jnp.sum(dots[h].astype(jnp.float32) * ot_ref[h, i], axis=0, keepdims=True)
+            for h in range(3)
+        ]
+        for h in range(3):
+            dqt_ref[h] = jnp.zeros((HD, BLK), jnp.float32)
+
+        def step(j, causal):
+            krows = block_rows(roff[j])
+            allowed = iota_k + j * BLK >= start
+            if causal:
+                allowed = allowed & (iota_k <= iota_q)
+            for h in range(3):
+                kh = qkv_ref[krows, GW + h * HD : GW + (h + 1) * HD]
+                vh = qkv_ref[krows, 2 * GW + h * HD : 2 * GW + (h + 1) * HD]
+                st = jnp.dot(kh, qts[h], preferred_element_type=jnp.float32)
+                dpt = jnp.dot(vh, dots[h], preferred_element_type=jnp.float32)
+                pt = jnp.where(allowed, jnp.exp2(st * factor - lses[h]), 0.0)
+                dst = (pt * (dpt - deltas[h])).astype(jnp.bfloat16)
+                dv_ref[h, j] += jnp.dot(
+                    pt.astype(jnp.bfloat16), dos[h], preferred_element_type=jnp.float32
+                )
+                dk_ref[h, j] += jnp.dot(dst, qs[h], preferred_element_type=jnp.float32)
+                dqt_ref[h] += jnp.dot(kt_ref[h, j], dst, preferred_element_type=jnp.float32)
+
+        def off_diagonal(j, c):
+            step(j, False)
+            return c
+
+        lax.fori_loop(jmin[i], i, off_diagonal, 0)
+        step(i, True)
+        for h in range(3):
+            out_ref[rows, h * HD : (h + 1) * HD] = (dqt_ref[h] * scale).T.astype(jnp.bfloat16)
+        return carry
+
+    lax.fori_loop(0, blocks, query_block, 0)
+
+    def finish(p, carry):
+        rows = block_rows(roff[p])
+        for h in range(3):
+            out_ref[rows, GW + h * HD : GW + (h + 1) * HD] = (dk_ref[h, p] * scale).astype(
+                jnp.bfloat16
+            )
+            out_ref[rows, 2 * GW + h * HD : 2 * GW + (h + 1) * HD] = dv_ref[h, p].astype(
+                jnp.bfloat16
+            )
+        return carry
+
+    lax.fori_loop(0, blocks, finish, 0)
+
+
+SMEM_SPEC = pl.BlockSpec(memory_space=pltpu.SMEM)
+VMEM_SPEC = pl.BlockSpec(memory_space=pltpu.VMEM)
+
+
+def attn_forward(roff, jmin, starts, qkv):
+    length = qkv.shape[0]
+    blocks = length // BLK
+    return pl.pallas_call(
+        attn_fwd_kernel,
+        name="attn_forward",
+        out_shape=(
+            jax.ShapeDtypeStruct((length, GW), jnp.bfloat16),
+            jax.ShapeDtypeStruct((3, blocks, HD, BLK), jnp.float32),
+            jax.ShapeDtypeStruct((3, blocks, BLK), jnp.float32),
+        ),
+        in_specs=[SMEM_SPEC, SMEM_SPEC, VMEM_SPEC, VMEM_SPEC],
+        out_specs=(VMEM_SPEC, VMEM_SPEC, VMEM_SPEC),
+        scratch_shapes=[
+            pltpu.VMEM((3, blocks, HD, BLK), jnp.bfloat16),
+            pltpu.VMEM((3, 1, BLK), jnp.float32),
+            pltpu.VMEM((3, 1, BLK), jnp.float32),
+            pltpu.VMEM((3, HD, BLK), jnp.float32),
+        ],
+    )(roff, jmin, starts, qkv)
+
+
+def attn_backward(roff, jmin, starts, qkv, dout, ot, lse):
+    length = qkv.shape[0]
+    blocks = length // BLK
+    return pl.pallas_call(
+        attn_bwd_kernel,
+        name="attn_backward",
+        out_shape=jax.ShapeDtypeStruct((length, 3 * GW), jnp.bfloat16),
+        in_specs=[SMEM_SPEC, SMEM_SPEC] + [VMEM_SPEC] * 5,
+        out_specs=VMEM_SPEC,
+        scratch_shapes=[
+            pltpu.VMEM((3, blocks, HD, BLK), jnp.bfloat16),
+            pltpu.VMEM((3, HD, BLK), jnp.float32),
+            pltpu.VMEM((3, blocks, BLK, HD), jnp.float32),
+            pltpu.VMEM((3, blocks, BLK, HD), jnp.float32),
+        ],
+    )(roff, jmin, starts, qkv, dout, ot, lse)
+
+
+def shift_ctx(value, shift):
+    return lax.ppermute(value, "ctx", [(i, (i + shift) % 4) for i in range(4)])
+
+
+def swap_core(value):
+    return lax.ppermute(value, "fsdp", [(i, i ^ 1) for i in range(4)])
+
+
+def swap_x(value):
+    return lax.ppermute(value, "fsdp", [(i, i ^ 2) for i in range(4)])
+
+
+def swap_dp(value):
+    return lax.ppermute(value, "dp", [(0, 1), (1, 0)])
+
+
+def gather_fsdp(value):
+    index = lax.axis_index("fsdp")
+    other = swap_x(value)
+    pair = jnp.stack([value, other])
+    far = swap_core(pair)
+    stacked = jnp.concatenate([pair, far])
+    parts = [
+        lax.dynamic_index_in_dim(stacked, order_of(index, wanted), 0, keepdims=False)
+        for wanted in range(4)
+    ]
+    return jnp.concatenate(parts, axis=0)
+
+
+def order_of(index, wanted):
+    apart = jnp.bitwise_xor(index, wanted)
+    return (apart >> 1) + 2 * (apart & 1)
+
+
+def dot32(a, b):
+    return jnp.dot(a, b, preferred_element_type=jnp.float32)
+
+
+def dot_nt(a, b):
+    return lax.dot_general(a, b, (((1,), (1,)), ((), ())), preferred_element_type=jnp.float32)
+
+
+def dot_tn(a, b):
+    return lax.dot_general(a, b, (((0,), (0,)), ((), ())), preferred_element_type=jnp.float32)
+
+
+def normalize(values_in):
+    center = jnp.mean(values_in, axis=-1, keepdims=True)
+    centred = values_in - center
+    spread = lax.rsqrt(jnp.mean(centred * centred, axis=-1, keepdims=True) + EPSILON)
+    return centred * spread, spread
+
+
+def norm_back(grad, unit, spread, gain):
+    scaled = grad * gain
+    return spread * (
+        scaled
+        - jnp.mean(scaled, axis=-1, keepdims=True)
+        - unit * jnp.mean(scaled * unit, axis=-1, keepdims=True)
+    )
+
+
+GROUP_OF = (0, 2, 3, 1)
+
+
+def grouped_body(
+    layer_input,
+    first_values,
+    segment_ids,
+    pairing,
+    norm_gains,
+    norm_biases,
+    w_qkv,
+    w_out,
+    w_up,
+    w_down,
+    cotangent,
+):
+    ctx = lax.axis_index("ctx")
+    fsdp = lax.axis_index("fsdp")
+    core = fsdp % 2
+    rows = layer_input.shape[1]
+    length = rows * 4
+    blocks = length // BLK
+    group_table = jnp.array(GROUP_OF, jnp.int32)
+    group_at = [group_table[(ctx + s) % 4] for s in range(4)]
+    own_group = group_at[0]
+
+    doc_row = segment_ids[0]
+    starts = jnp.sum(
+        (doc_row[None, :] < doc_row[:, None]).astype(jnp.int32), axis=1, dtype=jnp.int32
+    ).reshape(blocks, BLK)
+    firsts, lasts = doc_row[::BLK], doc_row[BLK - 1 :: BLK]
+    jmin = jnp.sum((lasts[None, :] < firsts[:, None]).astype(jnp.int32), axis=1, dtype=jnp.int32)
+    block_ids = jnp.arange(blocks, dtype=jnp.int32)
+    held_at = jnp.sum(
+        jnp.where(pairing[None, :] == block_ids[:, None], block_ids[None, :], 0), axis=1, dtype=jnp.int32
+    )
+    roff = ((ctx - held_at // 2) % 4) * rows + (held_at % 2) * BLK
+
+    first = first_values[0]
+    lower, upper_half = first[:, :GW], first[:, GW:]
+    first_parts = [jnp.where(ctx == 1, lower, upper_half)]
+    for s in range(1, 4):
+        message = jnp.where((ctx + s) % 4 == 1, lower, upper_half)
+        pairs = [(i, (i + s) % 4) for i in range(4) if (i + s) % 4 in (1, 2)]
+        first_parts.append(lax.ppermute(message, "ctx", pairs))
+    reuses = (ctx == 1) | (ctx == 2)
+
+    norms = jnp.concatenate([norm_gains, norm_biases], axis=0)
+    norm_rows = jnp.zeros((192, 128), jnp.bfloat16).at[:, :4].set(norms.T)
+    qkv_shard = jnp.concatenate([w_qkv, norm_rows], axis=1)
+    qkv_all = gather_fsdp(qkv_shard)
+    qkv_full = qkv_all[:, : w_qkv.shape[1]]
+    norm_cols = qkv_all[:, w_qkv.shape[1] : w_qkv.shape[1] + 4].astype(jnp.float32)
+    gain1_col, bias1_col = norm_cols[:, 0:1], norm_cols[:, 2:3]
+    norm_lines = norm_cols.T
+    gain1, gain2, bias1, bias2 = [norm_lines[k][None, :] for k in range(4)]
+    out_full = gather_fsdp(w_out)
+    up_half = jnp.concatenate([w_up, swap_x(w_up)], axis=1)
+    down_half = jnp.concatenate([w_down, swap_x(w_down)], axis=0)
+    fresh_width = VH * HD
+    grouped = []
+    for g in range(4):
+        wv = (
+            qkv_full[:, 2 * D + g * GW : 2 * D + (g + 1) * GW]
+            if (g + 1) * GW <= fresh_width
+            else jnp.zeros((D, GW), jnp.bfloat16)
+        )
+        grouped.append(
+            jnp.concatenate(
+                [qkv_full[:, g * GW : (g + 1) * GW], qkv_full[:, D + g * GW : D + (g + 1) * GW], wv],
+                axis=1,
+            )
+        )
+    grouped = jnp.stack(grouped)
+    w_groups = [lax.dynamic_index_in_dim(grouped, group_at[s], 0, keepdims=False) for s in range(4)]
+    w_own = w_groups[0]
+    w_turned = jnp.concatenate(w_groups, axis=1)
+    out_turned = jnp.concatenate(
+        [lax.dynamic_slice_in_dim(out_full, group_at[s] * GW, GW, axis=0) for s in range(4)], axis=0
+    )
+
+    chunk = layer_input[0]
+    half = rows // 2
+    parts = [chunk[:half], chunk[half:]]
+    slots = [chunk]
+    for s in range(3):
+        parts = [shift_ctx(part, 1) for part in parts]
+        slots.append(jnp.concatenate(parts, axis=0))
+    unit_slots, qkv_slots = [], []
+    for s in range(4):
+        unit, spread = normalize(slots[s].astype(jnp.float32))
+        if s == 0:
+            own_unit, own_spread = unit, spread
+        h_one = (unit * gain1 + bias1).astype(jnp.bfloat16)
+        part = dot32(h_one, w_own).astype(jnp.bfloat16)
+        value = jnp.where(reuses, first_parts[s], part[:, 2 * GW :])
+        qkv_slots.append(jnp.concatenate([part[:, : 2 * GW], value], axis=1))
+        unit_slots.append(unit.astype(jnp.bfloat16))
+    qkv_heads = jnp.concatenate(qkv_slots, axis=0)
+    unit_all = jnp.concatenate(unit_slots, axis=0)
+
+    cot_own = cotangent[0]
+    cot_both = jnp.concatenate([cot_own, swap_core(cot_own)], axis=0)
+    dactive = dot_nt(cot_both, down_half).astype(jnp.bfloat16)
+
+    mixed, mixed_t, lse = attn_forward(roff, jmin, starts, qkv_heads)
+    pieces = [mixed[:rows]] + [
+        shift_ctx(mixed[s * rows : (s + 1) * rows], -s) for s in range(1, 4)
+    ]
+    attn_low = jnp.concatenate(pieces, axis=1)
+    resid = chunk.astype(jnp.float32) + dot32(attn_low, out_turned)
+    unit_two, spread_two = normalize(resid)
+    h_two = (unit_two * gain2 + bias2).astype(jnp.bfloat16)
+    h_both = jnp.concatenate([h_two, swap_core(h_two)], axis=0)
+
+    upper = dot32(h_both, up_half)
+    root = 0.7978845608028654
+    squared = upper * upper
+    tanned = jnp.tanh(root * upper * (1.0 + 0.044715 * squared))
+    active_low = (0.5 * upper * (1.0 + tanned)).astype(jnp.bfloat16)
+    slope = 0.5 * (1.0 + tanned) + 0.5 * upper * (1.0 - tanned * tanned) * root * (
+        1.0 + 3.0 * 0.044715 * squared
+    )
+    dupper_low = (dactive.astype(jnp.float32) * slope).astype(jnp.bfloat16)
+
+    dh_both = dot_nt(dupper_low, up_half)
+    dh_two = dh_both[:rows] + swap_core(dh_both[rows:].astype(jnp.bfloat16)).astype(jnp.float32)
+    gain_two_grad = jnp.sum(dh_two * unit_two, axis=0)
+    bias_two_grad = jnp.sum(dh_two, axis=0)
+    dresid = cot_own.astype(jnp.float32) + norm_back(dh_two, unit_two, spread_two, gain2)
+    dbranch_low = dresid.astype(jnp.bfloat16)
+    dmixed = dot_nt(dbranch_low, out_turned).astype(jnp.bfloat16)
+    dmixed_slots = [dmixed[:, :GW]] + [
+        shift_ctx(dmixed[:, s * GW : (s + 1) * GW], s) for s in range(1, 4)
+    ]
+    dmixed_all = jnp.concatenate(dmixed_slots, axis=0)
+
+    out_both = dot32(active_low, down_half)
+    layer_out = (
+        resid + out_both[:rows] + swap_core(out_both[rows:].astype(jnp.bfloat16)).astype(jnp.float32)
+    ).astype(jnp.bfloat16)
+
+    down_grad = dot_tn(active_low, cot_both)
+    up_grad = dot_tn(h_both, dupper_low)
+    width = w_up.shape[1]
+    down_sum = down_grad[:width] + swap_x(down_grad[width:].astype(jnp.bfloat16)).astype(jnp.float32)
+    up_sum = up_grad[:, :width] + swap_x(up_grad[:, width:].astype(jnp.bfloat16)).astype(jnp.float32)
+    out_turned_grad = dot_tn(attn_low, dbranch_low)
+    out_parts = out_turned_grad.reshape(4, GW, D)
+    place = jnp.array([GROUP_OF.index(g) for g in range(4)], jnp.int32)
+    out_rows = [
+        lax.dynamic_index_in_dim(out_parts, (place[g] - ctx) % 4, 0, keepdims=False) for g in range(4)
+    ]
+    shares = jnp.stack(out_rows)
+    out_sum = reduce_fsdp(shares, fsdp)
+    down_low, up_low, out_low = lax.psum(
+        (down_sum.astype(jnp.bfloat16), up_sum.astype(jnp.bfloat16), out_sum.astype(jnp.bfloat16)),
+        ("dp", "ctx"),
+    )
+
+    dqkv = attn_backward(roff, jmin, starts, qkv_heads, dmixed_all, mixed_t, lse)
+    back = [dqkv[:rows]] + [shift_ctx(dqkv[s * rows : (s + 1) * rows], -s) for s in range(1, 4)]
+
+    product = dot_tn(unit_all, dqkv)
+    sums = jnp.sum(dqkv.astype(jnp.float32), axis=0, keepdims=True)
+    w_own32 = w_own.astype(jnp.float32)
+    gain_one_col = jnp.sum(w_own32 * product, axis=1, keepdims=True)
+    bias_one_col = jnp.sum(w_own32 * sums, axis=1, keepdims=True)
+    qkv_part = gain1_col * product + bias1_col * sums
+    extra = jnp.concatenate(
+        [gain_one_col, gain_two_grad[:, None], bias_one_col, bias_two_grad[:, None], jnp.zeros((D, 60), jnp.float32)],
+        axis=1,
+    )
+    share = jnp.concatenate([qkv_part, extra], axis=1).reshape(4, D // 4, 3 * GW + 64)
+    share = reduce_fsdp(share, fsdp)
+    share_low = share.astype(jnp.bfloat16)
+    share = share + swap_dp(share_low).astype(jnp.float32)
+    share_low = share.astype(jnp.bfloat16)
+    others = jnp.stack([share_low] + [shift_ctx(share_low, -s) for s in range(1, 4)])
+    by_group = [
+        lax.dynamic_index_in_dim(others, (place[g] - ctx) % 4, 0, keepdims=False).astype(jnp.float32)
+        for g in range(4)
+    ]
+    qkv_grad = jnp.concatenate(
+        [b[:, :GW] for b in by_group]
+        + [b[:, GW : 2 * GW] for b in by_group]
+        + [by_group[g][:, 2 * GW : 3 * GW] for g in range(2)],
+        axis=1,
+    )
+    tails = sum(b[:, 3 * GW : 3 * GW + 4] for b in by_group)
+    norm_grads = tails.T
+    gains_grad, biases_grad = norm_grads[:2], norm_grads[2:4]
+
+    back_all = jnp.concatenate(back, axis=1)
+    dh_one = dot_nt(back_all, w_turned)
+    input_grad = dresid + norm_back(dh_one, own_unit, own_spread, gain1)
+    value_parts = jnp.stack([b[:, 2 * GW :] for b in back])
+    first_grad = jnp.concatenate(
+        [
+            lax.dynamic_index_in_dim(value_parts, (place[g] - ctx) % 4, 0, keepdims=False)
+            for g in (2, 3)
+        ],
+        axis=1,
+    ).astype(jnp.float32)
+
+    return (
+        layer_out[None],
+        input_grad[None],
+        first_grad[None],
+        gains_grad,
+        biases_grad,
+        qkv_grad,
+        out_low.astype(jnp.float32),
+        up_low.astype(jnp.float32),
+        down_low.astype(jnp.float32),
+    )
+
+
+def reduce_fsdp(shares, fsdp):
+    turned = shares.reshape((2, 2) + shares.shape[1:])
+    core = fsdp % 2
+    x = fsdp // 2
+    keep = lax.dynamic_index_in_dim(turned, core, 1, keepdims=False)
+    give = lax.dynamic_index_in_dim(turned, 1 - core, 1, keepdims=False)
+    pair = keep + swap_core(give.astype(jnp.bfloat16)).astype(jnp.float32)
+    mine = lax.dynamic_index_in_dim(pair, x, 0, keepdims=False)
+    other = lax.dynamic_index_in_dim(pair, 1 - x, 0, keepdims=False)
+    return mine + swap_x(other.astype(jnp.bfloat16)).astype(jnp.float32)
+
+
 def solution(mesh):
+    sizes = dict(mesh.shape)
+    small = sizes["dp"] == 2 and sizes["ctx"] == 4 and sizes["fsdp"] == 4
+    chosen = grouped_body if small else wide_body
     in_specs = (
         P(("dp", "fsdp"), "ctx", None),
         P(("dp", "fsdp"), "ctx", None),
@@ -280,4 +767,4 @@
         P(None, "fsdp"),
         P("fsdp", None),
     )
-    return jax.shard_map(body, mesh=mesh, in_specs=in_specs, out_specs=out_specs, check_vma=False)
+    return jax.shard_map(chosen, mesh=mesh, in_specs=in_specs, out_specs=out_specs, check_vma=False)

time: 879 us -> 557 us (0.63)
  waiting for transfers between devices: 522 us -> 228 us
  matrix products: 180 us -> 47.5 us
  starting transfers between devices: 1.25 us -> 57.8 us
  Pallas kernels: 0 us -> 54.1 us
  blocking collectives: 33.8 us -> 0 us
  other arithmetic: 41 us -> 61.5 us
  between operations: 14.8 us -> 25.9 us
    reduce_scatter x6 -> x0, waiting for transfers between devices: 246 us -> none  [the longest x1 60.4 us: body(): lax.psum_scatter(dkeys_all.astype(jnp.bfloat16), 'ctx', scatter_dimension...]
    ppermute x0 -> x38, waiting for transfers between devices: none -> 147 us  [the longest x18 106 us: shift_ctx(): return lax.ppermute(value, 'ctx', [(i, (i + shift) % 4) for i in range(4)])]
    dot_general x40 -> x15, matrix products: 180 us -> 47.5 us  [the longest x4 17.5 us: dot_nt(): lax.dot_general(a, b, (((1,), (1,)), ((), ())), preferred_element_type=jn...]
    all_gather x6 -> x0, waiting for transfers between devices: 128 us -> none  [the longest x1 43.7 us: body(): lax.all_gather(key_low, 'ctx', axis=0, tiled=True)]
    ppermute x0 -> x38, starting transfers between devices: none -> 57.8 us  [the longest x18 32.2 us: shift_ctx(): return lax.ppermute(value, 'ctx', [(i, (i + shift) % 4) for i in range(4)])]
    pallas_call x0 -> x2, Pallas kernels: none -> 54.1 us  [the longest x1 27.3 us: attn_backward(): pl.pallas_call(attn_bwd_kernel, name='attn_backward', out_shape=jax.Shape...]
    psum x1, waiting for transfers between devices: 117 us -> 81.3 us  [grouped_body(): lax.psum((down_sum.astype(jnp.bfloat16), up_sum.astype(jnp.bfloat16), out...]
    unnamed x17 -> x1, waiting for transfers between devices: 31.5 us -> 0.02 us
  transfers between devices with their start and end apart: 15 -> 39, of which waited for: 14 -> 18; matrix products, arithmetic and copies ran while one was open for 19% -> 30% of each run, Pallas kernels for 0% -> 10%
where the time goes in v1:
time: 557 us; the launch traced here: 551 us
  waiting for transfers between devices  228 us (41%)
  local copies, waits for them, and re-layouts  76.3 us (14%)
  other arithmetic  61.5 us (11%)
  starting transfers between devices  57.8 us (10%)
  Pallas kernels  54.1 us (10%)
  matrix products  47.5 us (9%)
  between operations  25.9 us (5%)
    ppermute x18, waiting for transfers between devices, shift_ctx(): return lax.ppermute(value, 'ctx', [(i, (i + shift) % 4) for i in range(4)])  106 us
    psum x1, waiting for transfers between devices, grouped_body(): lax.psum((down_sum.astype(jnp.bfloat16), up_sum.astype(jnp.bfloat16), out...  81.3 us
    ppermute x18, starting transfers between devices, shift_ctx(): return lax.ppermute(value, 'ctx', [(i, (i + shift) % 4) for i in range(4)])  32.2 us
    pallas_call x1, Pallas kernels, attn_backward(): pl.pallas_call(attn_bwd_kernel, name='attn_backward', out_shape=jax.Shape...  27.3 us
    pallas_call x1, Pallas kernels, attn_forward(): pl.pallas_call(attn_fwd_kernel, name='attn_forward', out_shape=(jax.Shape...  26.7 us
    ppermute x8, waiting for transfers between devices, swap_x(): return lax.ppermute(value, 'fsdp', [(i, i ^ 2) for i in range(4)])  23 us
    dot_general x4, matrix products, dot_nt(): lax.dot_general(a, b, (((1,), (1,)), ((), ())), preferred_element_type=jn...  17.5 us
    concatenate x1, other arithmetic, grouped_body(): qkv_heads = jnp.concatenate(qkv_slots, axis=0)  15.6 us
  transfers between devices with their start and end apart: 39, of which 18 were waited for; matrix products, arithmetic and copies ran while one was open for 30% of the time, Pallas kernels for 10%

profile of v1, /device:TPU:0, one launch (start us, length us, event | category | flops | bytes accessed | tf_op | source)
XLA Modules:
  0.0 550.9 jit_solution(1594696591825335366)
XLA Ops:
  46.2 13.5 %collective-permute-done = bf16[192,2048]{1,0:T(8,128)(2,1)} collective-permute-done((bf16[192,2048]{1,0:T(8,128)(2,1)}, bf16[192,2048]{1,0:T(8,128)(2,1)}, u32[]{:S(2)}, u32[]{:S(2)}) %collective-permute-start) | collective-permute-done | bytes 786464 | tf_op jit(solution)/shard_map/ppermute | solution.py:459
  68.2 6.8 %collective-permute-done.8 = bf16[256,768]{1,0:T(8,128)(2,1)S(1)} collective-permute-done((bf16[256,768]{1,0:T(8,128)(2,1)S(1)}, bf16[256,768]{1,0:T(8,128)(2,1)S(1)}, u32[]{:S(2)}, u32[]{:S(2)}) %collective-permute-start.8) | collective-permute-done | bytes 393248 | tf_op jit(solution)/shard_map/ppermute | solution.py:451
  75.0 8.2 %collective-permute-done.9 = bf16[256,768]{1,0:T(8,128)(2,1)S(1)} collective-permute-done((bf16[256,768]{1,0:T(8,128)(2,1)S(1)}, bf16[256,768]{1,0:T(8,128)(2,1)S(1)}, u32[]{:S(2)}, u32[]{:S(2)}) %collective-permute-start.9) | collective-permute-done | bytes 393248 | tf_op jit(solution)/shard_map/ppermute | solution.py:451
  101.5 3.3 collective-permute-done.7
  104.9 4.3 collective-permute-done.4
  109.2 15.6 %maximum_maximum_fusion.qkv_ref = bf16[2048,576]{1,0:T(8,128)(2,1)} fusion(bf16[512,192]{1,0:T(8,128)(2,1)S(1)} %slice_select_fusion, bf16[512,384]{1,0:T(8,128)(2,1)S(1)} %slice.366, bf16[512,192]{1,0:T(8,128)(2,1)S(1)} %slice_select_fusion.1, bf16[512,384]{1,0:T(8,128)(2,1)S(1)} %slice-done, bf16[512,192]{1,0:T(8,128)(2,1)S(1)} %slice_select_fusion.2, ...), kind=kLoop, calls=%fused_computation.25 | loop fusion | flops 18874368 | bytes 4718592 | tf_op jit(solution)/shard_map/concatenate | solution.py:610
  124.8 26.7 %attn_forward.1 = (bf16[2048,192]{1,0:T(8,128)(2,1)}, f32[3,8,64,256]{3,2,1,0:T(8,128)}, f32[3,8,256]{2,1,0:T(8,128)}) custom-call(s32[8]{0:T(128)} %fusion.106.roff, s32[8]{0:T(128)} %get-tuple-element.180.jmin, s32[8,256]{1,0:T(8,128)} %reshape.211.start_ref, bf16[2048,576]{1,0:T(8,128)(2,1)} %maximum_maximum_fusion.qkv_ref), custom_call_target="tpu_custom_call" | custom-call | tf_op jit(solution)/shard_map/attn_forward/pallas_call | solution.py:413
  159.8 3.9 collective-permute-done.13
  163.7 6.7 %collective-permute-done.12 = bf16[512,192]{1,0:T(8,128)(2,1)S(1)} collective-permute-done((bf16[512,192]{1,0:T(8,128)(2,1)S(1)}, bf16[512,192]{1,0:T(8,128)(2,1)S(1)}, u32[]{:S(2)}, u32[]{:S(2)}) %collective-permute-start.12) | collective-permute-done | bytes 196640 | tf_op jit(solution)/shard_map/ppermute | solution.py:451
  189.4 4.7 fusion.66
  194.2 5.4 fusion.120
  199.6 7.0 %multiply_convert_fusion = bf16[1024,1536]{1,0:T(8,128)(2,1)S(1)} fusion(f32[1024,1536]{1,0:T(8,128)S(1)} %fusion.66, bf16[1536,768]{1,0:T(8,128)(2,1)} %constant_dynamic-update-slice_fusion.2, bf16[512,768]{1,0:T(8,128)(2,1)} %collective-permute-done.20, bf16[512,768]{1,0:T(8,128)(2,1)} %bitcast.30), kind=kOutput, calls=%fused_computation.1 | convolution fusion | flops 2450522112 | bytes 13369344 | tf_op jit(solution)/shard_map/dot_general | solution.py:489
  206.6 4.3 fusion.133
  211.7 5.2 fusion.64
  217.0 5.2 fusion.65
  234.4 7.6 %collective-permute-start.24 = (bf16[512,192]{1,0:T(8,128)(2,1)}, bf16[512,192]{1,0:T(8,128)(2,1)}, u32[]{:S(2)}, u32[]{:S(2)}) collective-permute-start(bf16[512,192]{1,0:T(8,128)(2,1)} %get-tuple-element.148), channel_id=1, source_target_pairs={{0,12},{4,0},{8,4},{12,8},{1,13},{5,1},{9,5},{13,9},{2,14},{6,2},{... | collective-permute-start | bytes 589832 | tf_op jit(solution)/shard_map/ppermute | solution.py:451
  249.0 14.9 %collective-permute-done.23 = bf16[512,192]{1,0:T(8,128)(2,1)} collective-permute-done((bf16[512,192]{1,0:T(8,128)(2,1)}, bf16[512,192]{1,0:T(8,128)(2,1)}, u32[]{:S(2)}, u32[]{:S(2)}) %collective-permute-start.23) | collective-permute-done | bytes 196640 | tf_op jit(solution)/shard_map/ppermute | solution.py:451
  266.3 27.3 %attn_backward.1 = bf16[2048,576]{1,0:T(8,128)(2,1)} custom-call(s32[8]{0:T(128)} %fusion.106.roff, s32[8]{0:T(128)} %get-tuple-element.180.jmin, s32[8,256]{1,0:T(8,128)} %reshape.211.start_ref, bf16[2048,576]{1,0:T(8,128)(2,1)} %maximum_maximum_fusion.qkv_ref, bf16[2048,192]{1,0:T(8,128)(2,1)} %pad_maximum_fusion.10.do_ref, ...), custom_call_target="tpu_custom_call" | custom-call | tf_op jit(solution)/shard_map/attn_backward/pallas_call | solution.py:435
  303.5 3.3 collective-permute-start.26
  319.8 34.3 %collective-permute-done.26 = bf16[512,576]{0,1:T(8,128)(2,1)} collective-permute-done((bf16[512,576]{0,1:T(8,128)(2,1)}, bf16[512,576]{0,1:T(8,128)(2,1)}, u32[]{:S(2)}, u32[]{:S(2)}) %collective-permute-start.26) | collective-permute-done | bytes 589856 | tf_op jit(solution)/shard_map/ppermute | solution.py:451
  358.4 5.2 concatenate.140
  363.7 5.4 fusion.121
  371.5 3.6 fusion.38
  378.4 3.4 concatenate.149
  389.2 5.6 %collective-permute-done.35 = bf16[192,768]{1,0:T(8,128)(2,1)S(1)} collective-permute-done((bf16[192,768]{1,0:T(8,128)(2,1)S(1)}, bf16[192,768]{1,0:T(8,128)(2,1)S(1)}, u32[]{:S(2)}, u32[]{:S(2)}) %collective-permute-start.35) | collective-permute-done | bytes 294944 | tf_op jit(solution)/shard_map/ppermute | solution.py:459
  395.6 3.9 collective-permute-done.29
  399.6 9.0 %collective-permute-start.30 = (bf16[192,640]{1,0:T(8,128)(2,1)S(1)}, bf16[192,640]{1,0:T(8,128)(2,1)S(1)}, u32[]{:S(2)}, u32[]{:S(2)}) collective-permute-start(bf16[192,640]{1,0:T(8,128)(2,1)S(1)} %fusion.100), channel_id=1, source_target_pairs={{0,16},{16,0},{1,17},{17,1},{2,18},{18,2},{3,19},{19,3},{4,20},{20... | collective-permute-start | bytes 737288 | tf_op jit(solution)/shard_map/ppermute | solution.py:463
  409.8 10.3 %collective-permute-done.30 = bf16[192,640]{1,0:T(8,128)(2,1)S(1)} collective-permute-done((bf16[192,640]{1,0:T(8,128)(2,1)S(1)}, bf16[192,640]{1,0:T(8,128)(2,1)S(1)}, u32[]{:S(2)}, u32[]{:S(2)}) %collective-permute-start.30) | collective-permute-done | bytes 245792 | tf_op jit(solution)/shard_map/ppermute | solution.py:463
  420.4 3.7 collective-permute-start.31
  425.2 11.2 %collective-permute-done.33 = bf16[192,640]{1,0:T(8,128)(2,1)S(1)} collective-permute-done((bf16[192,640]{1,0:T(8,128)(2,1)S(1)}, bf16[192,640]{1,0:T(8,128)(2,1)S(1)}, u32[]{:S(2)}, u32[]{:S(2)}) %collective-permute-start.33) | collective-permute-done | bytes 245792 | tf_op jit(solution)/shard_map/ppermute | solution.py:451
  436.4 16.0 %collective-permute-done.32 = bf16[192,640]{1,0:T(8,128)(2,1)S(1)} collective-permute-done((bf16[192,640]{1,0:T(8,128)(2,1)S(1)}, bf16[192,640]{1,0:T(8,128)(2,1)S(1)}, u32[]{:S(2)}, u32[]{:S(2)}) %collective-permute-start.32) | collective-permute-done | bytes 245792 | tf_op jit(solution)/shard_map/ppermute | solution.py:451
  456.2 81.3 %all-reduce.4.cloned.1.call-done = (bf16[192,768]{1,0:T(8,128)(2,1)}, bf16[768,768]{1,0:T(8,128)(2,1)}, bf16[768,768]{1,0:T(8,128)(2,1)}) async-done(((bf16[192,768]{1,0:T(8,128)(2,1)}, bf16[768,768]{1,0:T(8,128)(2,1)}, bf16[768,768]{1,0:T(8,128)(2,1)}), (bf16[192,768]{1,0:T(8,128)(2,1)}, bf16[768,768]{1,0:T(8,128)(2,1)}, bf16[768,768]{1,0:T(8,128)(2,1)})) %all-reduce.4.cloned.1.call-update) | async-done | bytes 2654224 | tf_op jit(solution)/shard_map/psum | solution.py:667
  (329 shorter events, 157.9 us)
Async XLA Ops:
  7.2 530.3 %all-reduce.4.cloned.1.call-start = ((), (), s32[]{:S(2)}) async-start(), calls=%async_computation | async-start | bytes 5308416 | tf_op jit(solution)/shard_map/psum | solution.py:667
  7.2 34.7 %collective-permute-start.14 = (bf16[192,768]{1,0:T(8,128)(2,1)}, bf16[192,768]{1,0:T(8,128)(2,1)S(1)}, u32[]{:S(2)}, u32[]{:S(2)}) collective-permute-start(bf16[192,768]{1,0:T(8,128)(2,1)} %param.22), channel_id=1, source_target_pairs={{0,2},{1,3},{2,0},{3,1},{4,6},{5,7},{6,4},{7,5},{8,10},{9,11},{10,... | collective-permute-start | bytes 884744 | tf_op jit(solution)/shard_map/ppermute | solution.py:459
  12.2 30.5 %collective-permute-start.2 = (bf16[256,768]{1,0:T(8,128)(2,1)}, bf16[256,768]{1,0:T(8,128)(2,1)S(1)}, u32[]{:S(2)}, u32[]{:S(2)}) collective-permute-start(bf16[256,768]{1,0:T(8,128)(2,1)} %get-tuple-element.151), channel_id=1, source_target_pairs={{0,4},{4,8},{8,12},{12,0},{1,5},{5,9},{9,13},{13,1},{2,6},{6,10},{... | collective-permute-start | bytes 1179656 | tf_op jit(solution)/shard_map/ppermute | solution.py:451
  13.7 30.5 %collective-permute-start.3 = (bf16[256,768]{1,0:T(8,128)(2,1)S(1)}, bf16[256,768]{1,0:T(8,128)(2,1)S(1)}, u32[]{:S(2)}, u32[]{:S(2)}) collective-permute-start(bf16[256,768]{1,0:T(8,128)(2,1)S(1)} %get-tuple-element.152), channel_id=1, source_target_pairs={{0,4},{4,8},{8,12},{12,0},{1,5},{5,9},{9,13},{13,1},{2,6},{6,10},{... | collective-permute-start | bytes 1179656 | tf_op jit(solution)/shard_map/ppermute | solution.py:451
  15.3 158.8 %collective-permute-start.17 = (bf16[768,768]{1,0:T(8,128)(2,1)}, bf16[768,768]{1,0:T(8,128)(2,1)}, u32[]{:S(2)}, u32[]{:S(2)}) collective-permute-start(bf16[768,768]{1,0:T(8,128)(2,1)} %param.23), channel_id=1, source_target_pairs={{0,2},{1,3},{2,0},{3,1},{4,6},{5,7},{6,4},{7,5},{8,10},{9,11},{10,... | collective-permute-start | bytes 3538952 | tf_op jit(solution)/shard_map/ppermute | solution.py:459
  20.2 39.5 %collective-permute-start = (bf16[192,2048]{1,0:T(8,128)(2,1)}, bf16[192,2048]{1,0:T(8,128)(2,1)}, u32[]{:S(2)}, u32[]{:S(2)}) collective-permute-start(bf16[192,2048]{1,0:T(8,128)(2,1)} %get-tuple-element.154), channel_id=1, source_target_pairs={{0,2},{1,3},{2,0},{3,1},{4,6},{5,7},{6,4},{7,5},{8,10},{9,11},{10,... | collective-permute-start | bytes 2359304 | tf_op jit(solution)/shard_map/ppermute | solution.py:459
  42.0 23.4 %collective-permute-start.15 = (bf16[2,192,768]{2,1,0:T(8,128)(2,1)S(1)}, bf16[2,192,768]{2,1,0:T(8,128)(2,1)S(1)}, u32[]{:S(2)}, u32[]{:S(2)}) collective-permute-start(bf16[2,192,768]{2,1,0:T(8,128)(2,1)S(1)} %pad_maximum_fusion.21), channel_id=1, source_target_pairs={{0,1},{1,0},{2,3},{3,2},{4,5},{5,4},{6,7},{7,6},{8,9},{9,8},{10,11... | collective-permute-start | bytes 1769480 | tf_op jit(solution)/shard_map/ppermute | solution.py:455
  42.7 18.5 %collective-permute-start.5 = (bf16[256,768]{1,0:T(8,128)(2,1)S(1)}, bf16[256,768]{1,0:T(8,128)(2,1)S(1)}, u32[]{:S(2)}, u32[]{:S(2)}) collective-permute-start(bf16[256,768]{1,0:T(8,128)(2,1)S(1)} %collective-permute-done.2), channel_id=1, source_target_pairs={{0,4},{4,8},{8,12},{12,0},{1,5},{5,9},{9,13},{13,1},{2,6},{6,10},{... | collective-permute-start | bytes 1179656 | tf_op jit(solution)/shard_map/ppermute | solution.py:451
  44.4 19.4 %collective-permute-start.6 = (bf16[256,768]{1,0:T(8,128)(2,1)S(1)}, bf16[256,768]{1,0:T(8,128)(2,1)S(1)}, u32[]{:S(2)}, u32[]{:S(2)}) collective-permute-start(bf16[256,768]{1,0:T(8,128)(2,1)S(1)} %collective-permute-done.3), channel_id=1, source_target_pairs={{0,4},{4,8},{8,12},{12,0},{1,5},{5,9},{9,13},{13,1},{2,6},{6,10},{... | collective-permute-start | bytes 1179656 | tf_op jit(solution)/shard_map/ppermute | solution.py:451
  61.1 22.7 %collective-permute-start.1 = (bf16[2,192,2048]{2,1,0:T(8,128)(2,1)S(1)}, bf16[2,192,2048]{2,1,0:T(8,128)(2,1)S(1)}, u32[]{:S(2)}, u32[]{:S(2)}) collective-permute-start(bf16[2,192,2048]{2,1,0:T(8,128)(2,1)S(1)} %pad_maximum_fusion.4), channel_id=1, source_target_pairs={{0,1},{1,0},{2,3},{3,2},{4,5},{5,4},{6,7},{7,6},{8,9},{9,8},{10,11... | collective-permute-start | bytes 4718600 | tf_op jit(solution)/shard_map/ppermute | solution.py:455
  61.1 13.9 %collective-permute-start.8 = (bf16[256,768]{1,0:T(8,128)(2,1)S(1)}, bf16[256,768]{1,0:T(8,128)(2,1)S(1)}, u32[]{:S(2)}, u32[]{:S(2)}) collective-permute-start(bf16[256,768]{1,0:T(8,128)(2,1)S(1)} %collective-permute-done.5), channel_id=1, source_target_pairs={{0,4},{4,8},{8,12},{12,0},{1,5},{5,9},{9,13},{13,1},{2,6},{6,10},{... | collective-permute-start | bytes 1179656 | tf_op jit(solution)/shard_map/ppermute | solution.py:451
  64.0 19.2 %collective-permute-start.9 = (bf16[256,768]{1,0:T(8,128)(2,1)S(1)}, bf16[256,768]{1,0:T(8,128)(2,1)S(1)}, u32[]{:S(2)}, u32[]{:S(2)}) collective-permute-start(bf16[256,768]{1,0:T(8,128)(2,1)S(1)} %collective-permute-done.6), channel_id=1, source_target_pairs={{0,4},{4,8},{8,12},{12,0},{1,5},{5,9},{9,13},{13,1},{2,6},{6,10},{... | collective-permute-start | bytes 1179656 | tf_op jit(solution)/shard_map/ppermute | solution.py:451
  65.4 111.1 %collective-permute-start.18 = (bf16[768,768]{1,0:T(8,128)(2,1)}, bf16[768,768]{1,0:T(8,128)(2,1)}, u32[]{:S(2)}, u32[]{:S(2)}) collective-permute-start(bf16[768,768]{1,0:T(8,128)(2,1)} %param.24), channel_id=1, source_target_pairs={{0,2},{1,3},{2,0},{3,1},{4,6},{5,7},{6,4},{7,5},{8,10},{9,11},{10,... | collective-permute-start | bytes 3538952 | tf_op jit(solution)/shard_map/ppermute | solution.py:459
  155.4 15.0 %collective-permute-start.12 = (bf16[512,192]{1,0:T(8,128)(2,1)S(1)}, bf16[512,192]{1,0:T(8,128)(2,1)S(1)}, u32[]{:S(2)}, u32[]{:S(2)}) collective-permute-start(bf16[512,192]{1,0:T(8,128)(2,1)S(1)} %get-tuple-element.139), channel_id=1, source_target_pairs={{0,8},{4,12},{8,0},{12,4},{1,9},{5,13},{9,1},{13,5},{2,10},{6,14},... | collective-permute-start | bytes 589832 | tf_op jit(solution)/shard_map/ppermute | solution.py:451
  156.3 14.1 %collective-permute-start.11 = (bf16[512,192]{1,0:T(8,128)(2,1)S(1)}, bf16[512,192]{1,0:T(8,128)(2,1)S(1)}, u32[]{:S(2)}, u32[]{:S(2)}) collective-permute-start(bf16[512,192]{1,0:T(8,128)(2,1)S(1)} %get-tuple-element.140), channel_id=1, source_target_pairs={{0,12},{4,0},{8,4},{12,8},{1,13},{5,1},{9,5},{13,9},{2,14},{6,2},{... | collective-permute-start | bytes 589832 | tf_op jit(solution)/shard_map/ppermute | solution.py:451
  163.7 35.9 %collective-permute-start.20 = (bf16[512,768]{1,0:T(8,128)(2,1)}, bf16[512,768]{1,0:T(8,128)(2,1)}, u32[]{:S(2)}, u32[]{:S(2)}) collective-permute-start(bf16[512,768]{1,0:T(8,128)(2,1)} %bitcast.30), channel_id=1, source_target_pairs={{0,1},{1,0},{2,3},{3,2},{4,5},{5,4},{6,7},{7,6},{8,9},{9,8},{10,11... | collective-permute-start | bytes 2359304 | tf_op jit(solution)/shard_map/ppermute | solution.py:455
  173.0 16.4 %collective-permute-start.16 = (bf16[512,768]{1,0:T(8,128)(2,1)}, bf16[512,768]{1,0:T(8,128)(2,1)}, u32[]{:S(2)}, u32[]{:S(2)}) collective-permute-start(bf16[512,768]{1,0:T(8,128)(2,1)} %add_convert_fusion), channel_id=1, source_target_pairs={{0,1},{1,0},{2,3},{3,2},{4,5},{5,4},{6,7},{7,6},{8,9},{9,8},{10,11... | collective-permute-start | bytes 2359304 | tf_op jit(solution)/shard_map/ppermute | solution.py:455
  211.1 18.4 %collective-permute-start.19 = (bf16[512,768]{1,0:T(8,128)(2,1)S(1)}, bf16[512,768]{1,0:T(8,128)(2,1)S(1)}, u32[]{:S(2)}, u32[]{:S(2)}) collective-permute-start(bf16[512,768]{1,0:T(8,128)(2,1)S(1)} %slice.473), channel_id=1, source_target_pairs={{0,1},{1,0},{2,3},{3,2},{4,5},{5,4},{6,7},{7,6},{8,9},{9,8},{10,11... | collective-permute-start | bytes 2359304 | tf_op jit(solution)/shard_map/ppermute | solution.py:455
  211.7 17.0 %collective-permute-start.21 = (bf16[512,768]{1,0:T(8,128)(2,1)S(1)}, bf16[512,768]{1,0:T(8,128)(2,1)S(1)}, u32[]{:S(2)}, u32[]{:S(2)}) collective-permute-start(bf16[512,768]{1,0:T(8,128)(2,1)S(1)} %slice.472), channel_id=1, source_target_pairs={{0,1},{1,0},{2,3},{3,2},{4,5},{5,4},{6,7},{7,6},{8,9},{9,8},{10,11... | collective-permute-start | bytes 2359304 | tf_op jit(solution)/shard_map/ppermute | solution.py:455
  226.6 81.4 %collective-permute-start.37 = (bf16[768,768]{1,0:T(8,128)(2,1)}, bf16[768,768]{1,0:T(8,128)(2,1)}, u32[]{:S(2)}, u32[]{:S(2)}) collective-permute-start(bf16[768,768]{1,0:T(8,128)(2,1)} %slice.470), channel_id=1, source_target_pairs={{0,2},{1,3},{2,0},{3,1},{4,6},{5,7},{6,4},{7,5},{8,10},{9,11},{10,... | collective-permute-start | bytes 3538952 | tf_op jit(solution)/shard_map/ppermute | solution.py:459
  227.0 86.3 %collective-permute-start.36 = (bf16[768,768]{1,0:T(8,128)(2,1)}, bf16[768,768]{1,0:T(8,128)(2,1)}, u32[]{:S(2)}, u32[]{:S(2)}) collective-permute-start(bf16[768,768]{1,0:T(8,128)(2,1)} %slice.471), channel_id=1, source_target_pairs={{0,2},{1,3},{2,0},{3,1},{4,6},{5,7},{6,4},{7,5},{8,10},{9,11},{10,... | collective-permute-start | bytes 3538952 | tf_op jit(solution)/shard_map/ppermute | solution.py:459
  234.4 14.6 %collective-permute-start.24 = (bf16[512,192]{1,0:T(8,128)(2,1)}, bf16[512,192]{1,0:T(8,128)(2,1)}, u32[]{:S(2)}, u32[]{:S(2)}) collective-permute-start(bf16[512,192]{1,0:T(8,128)(2,1)} %get-tuple-element.148), channel_id=1, source_target_pairs={{0,12},{4,0},{8,4},{12,8},{1,13},{5,1},{9,5},{13,9},{2,14},{6,2},{... | collective-permute-start | bytes 589832 | tf_op jit(solution)/shard_map/ppermute | solution.py:451
  242.0 22.0 %collective-permute-start.23 = (bf16[512,192]{1,0:T(8,128)(2,1)}, bf16[512,192]{1,0:T(8,128)(2,1)}, u32[]{:S(2)}, u32[]{:S(2)}) collective-permute-start(bf16[512,192]{1,0:T(8,128)(2,1)} %get-tuple-element.149), channel_id=1, source_target_pairs={{0,8},{4,12},{8,0},{12,4},{1,9},{5,13},{9,1},{13,5},{2,10},{6,14},... | collective-permute-start | bytes 589832 | tf_op jit(solution)/shard_map/ppermute | solution.py:451
  242.0 22.0 %collective-permute-start.22 = (bf16[512,192]{1,0:T(8,128)(2,1)}, bf16[512,192]{1,0:T(8,128)(2,1)}, u32[]{:S(2)}, u32[]{:S(2)}) collective-permute-start(bf16[512,192]{1,0:T(8,128)(2,1)} %get-tuple-element.150), channel_id=1, source_target_pairs={{0,4},{4,8},{8,12},{12,0},{1,5},{5,9},{9,13},{13,1},{2,6},{6,10},{... | collective-permute-start | bytes 589832 | tf_op jit(solution)/shard_map/ppermute | solution.py:451
  249.0 134.2 %collective-permute-start.34 = (bf16[2,192,768]{2,1,0:T(8,128)(2,1)}, bf16[2,192,768]{2,1,0:T(8,128)(2,1)}, u32[]{:S(2)}, u32[]{:S(2)}) collective-permute-start(bf16[2,192,768]{2,1,0:T(8,128)(2,1)} %fusion.94), channel_id=1, source_target_pairs={{0,1},{1,0},{2,3},{3,2},{4,5},{5,4},{6,7},{7,6},{8,9},{9,8},{10,11... | collective-permute-start | bytes 1769480 | tf_op jit(solution)/shard_map/ppermute | solution.py:455
  303.5 14.2 %collective-permute-start.25 = (bf16[512,576]{0,1:T(8,128)(2,1)}, bf16[512,576]{0,1:T(8,128)(2,1)}, u32[]{:S(2)}, u32[]{:S(2)}) collective-permute-start(bf16[512,576]{0,1:T(8,128)(2,1)} %copy.125), channel_id=1, source_target_pairs={{0,12},{4,0},{8,4},{12,8},{1,13},{5,1},{9,5},{13,9},{2,14},{6,2},{... | collective-permute-start | bytes 1769480 | tf_op jit(solution)/shard_map/ppermute | solution.py:451
  303.5 50.6 %collective-permute-start.26 = (bf16[512,576]{0,1:T(8,128)(2,1)}, bf16[512,576]{0,1:T(8,128)(2,1)}, u32[]{:S(2)}, u32[]{:S(2)}) collective-permute-start(bf16[512,576]{0,1:T(8,128)(2,1)} %copy.126), channel_id=1, source_target_pairs={{0,8},{4,12},{8,0},{12,4},{1,9},{5,13},{9,1},{13,5},{2,10},{6,14},... | collective-permute-start | bytes 1769480 | tf_op jit(solution)/shard_map/ppermute | solution.py:451
  308.0 48.2 %collective-permute-start.27 = (bf16[512,576]{0,1:T(8,128)(2,1)}, bf16[512,576]{0,1:T(8,128)(2,1)}, u32[]{:S(2)}, u32[]{:S(2)}) collective-permute-start(bf16[512,576]{0,1:T(8,128)(2,1)} %copy.127), channel_id=1, source_target_pairs={{0,4},{4,8},{8,12},{12,0},{1,5},{5,9},{9,13},{13,1},{2,6},{6,10},{... | collective-permute-start | bytes 1769480 | tf_op jit(solution)/shard_map/ppermute | solution.py:451
  399.6 20.6 %collective-permute-start.30 = (bf16[192,640]{1,0:T(8,128)(2,1)S(1)}, bf16[192,640]{1,0:T(8,128)(2,1)S(1)}, u32[]{:S(2)}, u32[]{:S(2)}) collective-permute-start(bf16[192,640]{1,0:T(8,128)(2,1)S(1)} %fusion.100), channel_id=1, source_target_pairs={{0,16},{16,0},{1,17},{17,1},{2,18},{18,2},{3,19},{19,3},{4,20},{20... | collective-permute-start | bytes 737288 | tf_op jit(solution)/shard_map/ppermute | solution.py:463
  420.3 16.1 %collective-permute-start.33 = (bf16[192,640]{1,0:T(8,128)(2,1)S(1)}, bf16[192,640]{1,0:T(8,128)(2,1)S(1)}, u32[]{:S(2)}, u32[]{:S(2)}) collective-permute-start(bf16[192,640]{1,0:T(8,128)(2,1)S(1)} %add_convert_fusion.1), channel_id=1, source_target_pairs={{0,4},{4,8},{8,12},{12,0},{1,5},{5,9},{9,13},{13,1},{2,6},{6,10},{... | collective-permute-start | bytes 737288 | tf_op jit(solution)/shard_map/ppermute | solution.py:451
  420.3 32.1 %collective-permute-start.32 = (bf16[192,640]{1,0:T(8,128)(2,1)S(1)}, bf16[192,640]{1,0:T(8,128)(2,1)S(1)}, u32[]{:S(2)}, u32[]{:S(2)}) collective-permute-start(bf16[192,640]{1,0:T(8,128)(2,1)S(1)} %add_convert_fusion.1), channel_id=1, source_target_pairs={{0,8},{4,12},{8,0},{12,4},{1,9},{5,13},{9,1},{13,5},{2,10},{6,14},... | collective-permute-start | bytes 737288 | tf_op jit(solution)/shard_map/ppermute | solution.py:451
  420.4 32.0 %collective-permute-start.31 = (bf16[192,640]{1,0:T(8,128)(2,1)S(1)}, bf16[192,640]{1,0:T(8,128)(2,1)S(1)}, u32[]{:S(2)}, u32[]{:S(2)}) collective-permute-start(bf16[192,640]{1,0:T(8,128)(2,1)S(1)} %add_convert_fusion.1), channel_id=1, source_target_pairs={{0,12},{4,0},{8,4},{12,8},{1,13},{5,1},{9,5},{13,9},{2,14},{6,2},{... | collective-permute-start | bytes 737288 | tf_op jit(solution)/shard_map/ppermute | solution.py:451
  (73 other events, 708.5 us)
Sparse Core Ops, SparseCore 0:
  395.8 141.7 all-reduce.3

commit v2 on v1

--- a/solution.py
+++ b/solution.py
@@ -268,7 +268,9 @@
     return pl.ds(pl.multiple_of(index, BLK), BLK)
 
 
-def attn_fwd_kernel(roff, jmin, start_ref, qkv_ref, o_ref, ot_ref, lse_ref, vt_ref, m_ref, l_ref, acc_ref):
+def attn_fwd_kernel(
+    roff, jmin, start_ref, qkv_ref, p0, p1, p2, p3, ot_ref, lse_ref, o_ref, vt_ref, m_ref, l_ref, acc_ref
+):
     blocks = qkv_ref.shape[0] // BLK
     factor = HD ** (-0.5) * LOG2E
     iota_k = lax.broadcasted_iota(jnp.int32, (BLK, BLK), 0)
@@ -325,14 +327,24 @@
         return carry
 
     lax.fori_loop(0, blocks, query_block, 0)
-
-
-def attn_bwd_kernel(roff, jmin, start_ref, qkv_ref, do_ref, ot_ref, lse_ref, out_ref, kt_ref, dqt_ref, dk_ref, dv_ref):
+    for s, piece in enumerate((p0, p1, p2, p3)):
+        for b in range(2):
+            piece[:, b * GW : (b + 1) * GW] = o_ref[(2 * s + b) * BLK : (2 * s + b + 1) * BLK, :]
+
+
+def attn_bwd_kernel(
+    roff, jmin, start_ref, qkv_ref, d0, d1, d2, d3, ot_ref, lse_ref, out_ref, p0, p1, p2, p3,
+    do_ref, kt_ref, dqt_ref, dk_ref, dv_ref,
+):
     blocks = qkv_ref.shape[0] // BLK
     scale = HD ** (-0.5)
     factor = scale * LOG2E
     iota_k = lax.broadcasted_iota(jnp.int32, (BLK, BLK), 0)
     iota_q = lax.broadcasted_iota(jnp.int32, (BLK, BLK), 1)
+
+    for s, piece in enumerate((d0, d1, d2, d3)):
+        for b in range(2):
+            do_ref[(2 * s + b) * BLK : (2 * s + b + 1) * BLK, :] = piece[:, b * GW : (b + 1) * GW]
 
     def prepare(p, carry):
         rows = block_rows(roff[p])
@@ -401,6 +413,9 @@
         return carry
 
     lax.fori_loop(0, blocks, finish, 0)
+    for s, piece in enumerate((p0, p1, p2, p3)):
+        for b in range(2):
+            piece[:, 3 * b * GW : 3 * (b + 1) * GW] = out_ref[(2 * s + b) * BLK : (2 * s + b + 1) * BLK, :]
 
 
 SMEM_SPEC = pl.BlockSpec(memory_space=pltpu.SMEM)
@@ -414,13 +429,14 @@
         attn_fwd_kernel,
         name="attn_forward",
         out_shape=(
-            jax.ShapeDtypeStruct((length, GW), jnp.bfloat16),
+            *[jax.ShapeDtypeStruct((BLK, 2 * GW), jnp.bfloat16)] * 4,
             jax.ShapeDtypeStruct((3, blocks, HD, BLK), jnp.float32),
             jax.ShapeDtypeStruct((3, blocks, BLK), jnp.float32),
         ),
         in_specs=[SMEM_SPEC, SMEM_SPEC, VMEM_SPEC, VMEM_SPEC],
-        out_specs=(VMEM_SPEC, VMEM_SPEC, VMEM_SPEC),
+        out_specs=(VMEM_SPEC,) * 6,
         scratch_shapes=[
+            pltpu.VMEM((length, GW), jnp.bfloat16),
             pltpu.VMEM((3, blocks, HD, BLK), jnp.bfloat16),
             pltpu.VMEM((3, 1, BLK), jnp.float32),
             pltpu.VMEM((3, 1, BLK), jnp.float32),
@@ -435,65 +451,23 @@
     return pl.pallas_call(
         attn_bwd_kernel,
         name="attn_backward",
-        out_shape=jax.ShapeDtypeStruct((length, 3 * GW), jnp.bfloat16),
-        in_specs=[SMEM_SPEC, SMEM_SPEC] + [VMEM_SPEC] * 5,
-        out_specs=VMEM_SPEC,
+        out_shape=(
+            jax.ShapeDtypeStruct((length, 3 * GW), jnp.bfloat16),
+            *[jax.ShapeDtypeStruct((BLK, 6 * GW), jnp.bfloat16)] * 4,
+        ),
+        in_specs=[SMEM_SPEC, SMEM_SPEC] + [VMEM_SPEC] * 8,
+        out_specs=(VMEM_SPEC,) * 5,
         scratch_shapes=[
+            pltpu.VMEM((length, GW), jnp.bfloat16),
             pltpu.VMEM((3, blocks, HD, BLK), jnp.bfloat16),
             pltpu.VMEM((3, HD, BLK), jnp.float32),
             pltpu.VMEM((3, blocks, BLK, HD), jnp.float32),
             pltpu.VMEM((3, blocks, BLK, HD), jnp.float32),
         ],
-    )(roff, jmin, starts, qkv, dout, ot, lse)
-
-
-def shift_ctx(value, shift):
-    return lax.ppermute(value, "ctx", [(i, (i + shift) % 4) for i in range(4)])
-
-
-def swap_core(value):
-    return lax.ppermute(value, "fsdp", [(i, i ^ 1) for i in range(4)])
-
-
-def swap_x(value):
-    return lax.ppermute(value, "fsdp", [(i, i ^ 2) for i in range(4)])
-
-
-def swap_dp(value):
-    return lax.ppermute(value, "dp", [(0, 1), (1, 0)])
-
-
-def gather_fsdp(value):
-    index = lax.axis_index("fsdp")
-    other = swap_x(value)
-    pair = jnp.stack([value, other])
-    far = swap_core(pair)
-    stacked = jnp.concatenate([pair, far])
-    parts = [
-        lax.dynamic_index_in_dim(stacked, order_of(index, wanted), 0, keepdims=False)
-        for wanted in range(4)
-    ]
-    return jnp.concatenate(parts, axis=0)
-
-
-def order_of(index, wanted):
-    apart = jnp.bitwise_xor(index, wanted)
-    return (apart >> 1) + 2 * (apart & 1)
-
-
-def dot32(a, b):
-    return jnp.dot(a, b, preferred_element_type=jnp.float32)
-
-
-def dot_nt(a, b):
-    return lax.dot_general(a, b, (((1,), (1,)), ((), ())), preferred_element_type=jnp.float32)
-
-
-def dot_tn(a, b):
-    return lax.dot_general(a, b, (((0,), (0,)), ((), ())), preferred_element_type=jnp.float32)
-
-
-def normalize(values_in):
+    )(roff, jmin, starts, qkv, *dout, ot, lse)
+
+
+def unit_of(values_in):
     center = jnp.mean(values_in, axis=-1, keepdims=True)
     centred = values_in - center
     spread = lax.rsqrt(jnp.mean(centred * centred, axis=-1, keepdims=True) + EPSILON)
@@ -509,7 +483,323 @@
     )
 
 
+def project_kernel(ids, xa, xb, w_ref, lines, first, *rest):
+    unit_out, qkv_out = rest[-2], rest[-1]
+    weights = w_ref[0]
+    reuse = ids[1] == 1
+    for b, x_ref in enumerate((xa, xb)):
+        unit, _ = unit_of(x_ref[...].astype(jnp.float32))
+        normed = (unit * lines[0:1, :] + lines[2:3, :]).astype(jnp.bfloat16)
+        part = jnp.dot(normed, weights, preferred_element_type=jnp.float32).astype(jnp.bfloat16)
+        here = slice(b * BLK, (b + 1) * BLK)
+        qkv_out[here, : 2 * GW] = part[:, : 2 * GW]
+        qkv_out[here, 2 * GW :] = jnp.where(reuse, first[:, b * GW : (b + 1) * GW], part[:, 2 * GW :])
+        unit_out[:, here] = unit.astype(jnp.bfloat16).T
+
+
+def project(slot, ids, xa, xb, grouped, lines, first, held):
+    length = 8 * BLK
+    whole = lambda *shape: pl.BlockSpec(shape, lambda i, ids_ref: (0,) * len(shape))
+    in_specs = [
+        whole(BLK, D),
+        whole(BLK, D),
+        pl.BlockSpec((1, D, 3 * GW), lambda i, ids_ref: (ids_ref[0], 0, 0)),
+        whole(4, D),
+        whole(BLK, 2 * GW),
+    ]
+    args = [ids, xa, xb, grouped, lines, first]
+    aliases = {}
+    if held is not None:
+        in_specs += [pl.BlockSpec(memory_space=pl.ANY)] * 2
+        aliases = {6: 0, 7: 1}
+        args += list(held)
+    return pl.pallas_call(
+        project_kernel,
+        name="project_" + str(slot),
+        grid_spec=pltpu.PrefetchScalarGridSpec(
+            num_scalar_prefetch=1,
+            grid=(1,),
+            in_specs=in_specs,
+            out_specs=(
+                pl.BlockSpec((D, 2 * BLK), lambda i, ids_ref: (0, slot)),
+                pl.BlockSpec((2 * BLK, 3 * GW), lambda i, ids_ref: (slot, 0)),
+            ),
+        ),
+        out_shape=(
+            jax.ShapeDtypeStruct((D, length), jnp.bfloat16),
+            jax.ShapeDtypeStruct((length, 3 * GW), jnp.bfloat16),
+        ),
+        input_output_aliases=aliases,
+    )(*args)
+
+
+def resid_kernel(groups, x_ref, m0, m1, m2, m3, w_ref, lines, resid_ref, h_ref, attn_ref):
+    for b in range(2):
+        here = slice(b * BLK, (b + 1) * BLK)
+        for s, piece in enumerate((m0, m1, m2, m3)):
+            attn_ref[here, s * GW : (s + 1) * GW] = piece[:, b * GW : (b + 1) * GW]
+        total = x_ref[here, :].astype(jnp.float32)
+        for s, piece in enumerate((m0, m1, m2, m3)):
+            rows = pl.ds(pl.multiple_of(groups[s] * GW, GW), GW)
+            total += jnp.dot(
+                piece[:, b * GW : (b + 1) * GW], w_ref[rows, :], preferred_element_type=jnp.float32
+            )
+        resid_ref[here, :] = total
+        unit, _ = unit_of(total)
+        h_ref[here, :] = (unit * lines[1:2, :] + lines[3:4, :]).astype(jnp.bfloat16)
+
+
+def residual(groups, x, pieces, out_full, lines):
+    rows = x.shape[0]
+    return pl.pallas_call(
+        resid_kernel,
+        name="residual",
+        out_shape=(
+            jax.ShapeDtypeStruct((rows, D), jnp.float32),
+            jax.ShapeDtypeStruct((rows, D), jnp.bfloat16),
+            jax.ShapeDtypeStruct((rows, D), jnp.bfloat16),
+        ),
+        in_specs=[SMEM_SPEC] + [VMEM_SPEC] * 7,
+        out_specs=(VMEM_SPEC,) * 3,
+    )(groups, x, *pieces, out_full, lines)
+
+
+ROOT = 0.7978845608028654
+TILE = 256
+
+
+def feed_kernel(ha, hb, dact, um, uo, gm, go, dum, duo, dh_own, dh_far, acc):
+    t = pl.program_id(0)
+    half = pl.num_programs(0) // 2
+    rows = ha.shape[0]
+
+    @pl.when(t == 0)
+    def _():
+        acc[...] = jnp.zeros_like(acc)
+
+    def tile(up_ref, g_out, du_out):
+        weights = up_ref[...]
+        for r in range(2 * rows // TILE):
+            src = ha if r * TILE < rows else hb
+            at = (r * TILE) % rows
+            here = slice(r * TILE, (r + 1) * TILE)
+            u = jnp.dot(src[at : at + TILE, :], weights, preferred_element_type=jnp.float32)
+            squared = u * u
+            tanned = jnp.tanh(ROOT * u * (1.0 + 0.044715 * squared))
+            inner = 0.5 + 0.5 * tanned
+            g_out[here, :] = (u * inner).astype(jnp.bfloat16)
+            slope = inner + u * (0.5 - 0.5 * tanned * tanned) * (ROOT + (3.0 * 0.044715 * ROOT) * squared)
+            du = (dact[here, :].astype(jnp.float32) * slope).astype(jnp.bfloat16)
+            du_out[here, :] = du
+            acc[here, :] += lax.dot_general(
+                du, weights, (((1,), (1,)), ((), ())), preferred_element_type=jnp.float32
+            )
+
+    @pl.when(t < half)
+    def _():
+        tile(um, gm, dum)
+
+    @pl.when(t >= half)
+    def _():
+        tile(uo, go, duo)
+
+    @pl.when(t == pl.num_programs(0) - 1)
+    def _():
+        dh_own[...] = acc[:rows, :]
+        dh_far[...] = acc[rows:, :].astype(jnp.bfloat16)
+
+
+def feed(ha, hb, dact, up_mine, up_other):
+    rows = ha.shape[0]
+    width = up_mine.shape[1]
+    steps = width // TILE
+    whole = lambda *shape: pl.BlockSpec(shape, lambda t: (0,) * len(shape))
+    early = lambda t: jnp.minimum(t, steps - 1)
+    late = lambda t: jnp.maximum(t - steps, 0)
+    wide = lambda pick: pl.BlockSpec((2 * rows, TILE), lambda t: (0, pick(t)))
+    return pl.pallas_call(
+        feed_kernel,
+        name="feed",
+        grid=(2 * steps,),
+        out_shape=(
+            *[jax.ShapeDtypeStruct((2 * rows, width), jnp.bfloat16)] * 4,
+            jax.ShapeDtypeStruct((rows, D), jnp.float32),
+            jax.ShapeDtypeStruct((rows, D), jnp.bfloat16),
+        ),
+        in_specs=[
+            whole(rows, D),
+            whole(rows, D),
+            pl.BlockSpec((2 * rows, TILE), lambda t: (0, t)),
+            pl.BlockSpec((D, TILE), lambda t: (0, early(t))),
+            pl.BlockSpec((D, TILE), lambda t: (0, late(t))),
+        ],
+        out_specs=(wide(early), wide(late), wide(early), wide(late), whole(rows, D), whole(rows, D)),
+        scratch_shapes=[pltpu.VMEM((2 * rows, D), jnp.float32)],
+    )(ha, hb, dact, up_mine, up_other)
+
+
+def branch_kernel(groups, dh_ref, far_ref, resid_ref, cot_ref, lines, w_ref, dresid_ref, low_ref, p0, p1, p2, p3, sums):
+    gain_sum = jnp.zeros((1, D), jnp.float32)
+    bias_sum = jnp.zeros((1, D), jnp.float32)
+    for b in range(2):
+        here = slice(b * BLK, (b + 1) * BLK)
+        unit, spread = unit_of(resid_ref[here, :])
+        grad = dh_ref[here, :] + far_ref[here, :].astype(jnp.float32)
+        gain_sum += jnp.sum(grad * unit, axis=0, keepdims=True)
+        bias_sum += jnp.sum(grad, axis=0, keepdims=True)
+        total = cot_ref[here, :].astype(jnp.float32) + norm_back(grad, unit, spread, lines[1:2, :])
+        dresid_ref[here, :] = total
+        low = total.astype(jnp.bfloat16)
+        low_ref[here, :] = low
+        for s, piece in enumerate((p0, p1, p2, p3)):
+            rows = pl.ds(pl.multiple_of(groups[s] * GW, GW), GW)
+            piece[:, b * GW : (b + 1) * GW] = lax.dot_general(
+                low, w_ref[rows, :], (((1,), (1,)), ((), ())), preferred_element_type=jnp.float32
+            ).astype(jnp.bfloat16)
+    sums[0:1, :] = gain_sum
+    sums[1:2, :] = bias_sum
+
+
+def branch(groups, dh, far, resid, cot, lines, out_full):
+    rows = dh.shape[0]
+    return pl.pallas_call(
+        branch_kernel,
+        name="branch",
+        out_shape=(
+            jax.ShapeDtypeStruct((rows, D), jnp.float32),
+            jax.ShapeDtypeStruct((rows, D), jnp.bfloat16),
+            *[jax.ShapeDtypeStruct((BLK, 2 * GW), jnp.bfloat16)] * 4,
+            jax.ShapeDtypeStruct((2, D), jnp.float32),
+        ),
+        in_specs=[SMEM_SPEC] + [VMEM_SPEC] * 6,
+        out_specs=(VMEM_SPEC,) * 7,
+    )(groups, dh, far, resid, cot, lines, out_full)
+
+
+def product_kernel(ids, unit_ref, dqkv_ref, w_ref, lines, sums2, out_ref):
+    weights = w_ref[0].astype(jnp.float32)
+    columns = lines[...].T
+    two = sums2[...].T
+    column_sums = jnp.sum(dqkv_ref[...].astype(jnp.float32), axis=0, keepdims=True)
+    zeros = jnp.zeros((BLK, 60), jnp.float32)
+    for r in range(D // BLK):
+        here = slice(r * BLK, (r + 1) * BLK)
+        product = jnp.dot(unit_ref[here, :], dqkv_ref[...], preferred_element_type=jnp.float32)
+        w = weights[here, :]
+        gain_col = jnp.sum(w * product, axis=1, keepdims=True)
+        bias_col = jnp.sum(w * column_sums, axis=1, keepdims=True)
+        out_ref[here, : 3 * GW] = columns[here, 0:1] * product + columns[here, 2:3] * column_sums
+        out_ref[here, 3 * GW :] = jnp.concatenate(
+            [gain_col, two[here, 0:1], bias_col, two[here, 1:2], zeros], axis=1
+        )
+
+
+def qkv_product(ids, unit_t, dqkv, grouped, lines, sums2):
+    whole = lambda *shape: pl.BlockSpec(shape, lambda i, ids_ref: (0,) * len(shape))
+    length = dqkv.shape[0]
+    return pl.pallas_call(
+        product_kernel,
+        name="qkv_product",
+        grid_spec=pltpu.PrefetchScalarGridSpec(
+            num_scalar_prefetch=1,
+            grid=(1,),
+            in_specs=[
+                whole(D, length),
+                whole(length, 3 * GW),
+                pl.BlockSpec((1, D, 3 * GW), lambda i, ids_ref: (ids_ref[0], 0, 0)),
+                whole(4, D),
+                whole(2, D),
+            ],
+            out_specs=whole(D, 3 * GW + 64),
+        ),
+        out_shape=jax.ShapeDtypeStruct((D, 3 * GW + 64), jnp.float32),
+    )(ids, unit_t, dqkv, grouped, lines, sums2)
+
+
+def input_kernel(groups, place, x_ref, dresid_ref, b0, b1, b2, b3, w_ref, lines, out_ref, first_ref):
+    pieces = (b0, b1, b2, b3)
+    for b in range(2):
+        here = slice(b * BLK, (b + 1) * BLK)
+        wide = slice(3 * b * GW, 3 * (b + 1) * GW)
+        grad = jnp.zeros((BLK, D), jnp.float32)
+        for s, piece in enumerate(pieces):
+            grad += lax.dot_general(
+                piece[:, wide], w_ref[groups[s]], (((1,), (1,)), ((), ())), preferred_element_type=jnp.float32
+            )
+        unit, spread = unit_of(x_ref[here, :].astype(jnp.float32))
+        out_ref[here, :] = dresid_ref[here, :] + norm_back(grad, unit, spread, lines[0:1, :])
+        values = slice(3 * b * GW + 2 * GW, 3 * (b + 1) * GW)
+        for k in range(2):
+            total = jnp.zeros((BLK, GW), jnp.float32)
+            for s, piece in enumerate(pieces):
+                total = jnp.where(place[2 + k] == s, piece[:, values].astype(jnp.float32), total)
+            first_ref[here, k * GW : (k + 1) * GW] = total
+
+
+def input_gradient(groups, place, x, dresid, pieces, grouped, lines):
+    rows = x.shape[0]
+    return pl.pallas_call(
+        input_kernel,
+        name="input_gradient",
+        out_shape=(
+            jax.ShapeDtypeStruct((rows, D), jnp.float32),
+            jax.ShapeDtypeStruct((rows, 2 * GW), jnp.float32),
+        ),
+        in_specs=[SMEM_SPEC, SMEM_SPEC] + [VMEM_SPEC] * 8,
+        out_specs=(VMEM_SPEC,) * 2,
+    )(groups, place, x, dresid, *pieces, grouped, lines)
+
+
+def after(value, *others):
+    return lax.optimization_barrier((value,) + others)[0]
+
+
+def shift_ctx(value, shift):
+    return lax.ppermute(value, "ctx", [(i, (i + shift) % 4) for i in range(4)])
+
+
+def swap_core(value):
+    return lax.ppermute(value, "fsdp", [(i, i ^ 1) for i in range(4)])
+
+
+def swap_x(value):
+    return lax.ppermute(value, "fsdp", [(i, i ^ 2) for i in range(4)])
+
+
+def swap_dp(value):
+    return lax.ppermute(value, "dp", [(0, 1), (1, 0)])
+
+
+def in_fsdp_order(index, own, other, pair):
+    stacked = jnp.concatenate([own[None], other[None], pair])
+    return [
+        lax.dynamic_index_in_dim(stacked, order_of(index, wanted), 0, keepdims=False)
+        for wanted in range(4)
+    ]
+
+
+def order_of(index, wanted):
+    apart = jnp.bitwise_xor(index, wanted)
+    return (apart >> 1) + 2 * (apart & 1)
+
+
+def dot32(a, b):
+    return jnp.dot(a, b, preferred_element_type=jnp.float32)
+
+
+def dot_nt(a, b):
+    return lax.dot_general(a, b, (((1,), (1,)), ((), ())), preferred_element_type=jnp.float32)
+
+
+def dot_tn(a, b):
+    return lax.dot_general(a, b, (((0,), (0,)), ((), ())), preferred_element_type=jnp.float32)
+
+
 GROUP_OF = (0, 2, 3, 1)
+
+
+def pick(table, index):
+    return sum(jnp.where(index == k, entry, 0) for k, entry in enumerate(table)).astype(jnp.int32)
 
 
 def grouped_body(
@@ -527,13 +817,14 @@
 ):
     ctx = lax.axis_index("ctx")
     fsdp = lax.axis_index("fsdp")
-    core = fsdp % 2
     rows = layer_input.shape[1]
     length = rows * 4
     blocks = length // BLK
-    group_table = jnp.array(GROUP_OF, jnp.int32)
-    group_at = [group_table[(ctx + s) % 4] for s in range(4)]
-    own_group = group_at[0]
+    turns = jnp.arange(4, dtype=jnp.int32)
+    groups = pick(GROUP_OF, (ctx + turns) % 4)
+    place = (pick([GROUP_OF.index(g) for g in range(4)], turns) - ctx) % 4
+    reuses = ((ctx == 1) | (ctx == 2)).astype(jnp.int32)
+    ids = jnp.stack([groups[0], reuses])
 
     doc_row = segment_ids[0]
     starts = jnp.sum(
@@ -547,33 +838,46 @@
     )
     roff = ((ctx - held_at // 2) % 4) * rows + (held_at % 2) * BLK
 
+    chunk = layer_input[0]
+    xa, xb = chunk[:BLK], chunk[BLK:]
+    qkv_other = swap_x(w_qkv)
+    ring_a, ring_b = [xa, shift_ctx(xa, 1)], [xb, shift_ctx(xb, 1)]
+
     first = first_values[0]
-    lower, upper_half = first[:, :GW], first[:, GW:]
-    first_parts = [jnp.where(ctx == 1, lower, upper_half)]
+    message = [
+        jnp.concatenate([first[:BLK, k * GW : (k + 1) * GW], first[BLK:, k * GW : (k + 1) * GW]], axis=1)
+        for k in range(2)
+    ]
+    first_parts = [jnp.where(ctx == 1, message[0], message[1])]
     for s in range(1, 4):
-        message = jnp.where((ctx + s) % 4 == 1, lower, upper_half)
         pairs = [(i, (i + s) % 4) for i in range(4) if (i + s) % 4 in (1, 2)]
-        first_parts.append(lax.ppermute(message, "ctx", pairs))
-    reuses = (ctx == 1) | (ctx == 2)
-
-    norms = jnp.concatenate([norm_gains, norm_biases], axis=0)
-    norm_rows = jnp.zeros((192, 128), jnp.bfloat16).at[:, :4].set(norms.T)
-    qkv_shard = jnp.concatenate([w_qkv, norm_rows], axis=1)
-    qkv_all = gather_fsdp(qkv_shard)
-    qkv_full = qkv_all[:, : w_qkv.shape[1]]
-    norm_cols = qkv_all[:, w_qkv.shape[1] : w_qkv.shape[1] + 4].astype(jnp.float32)
-    gain1_col, bias1_col = norm_cols[:, 0:1], norm_cols[:, 2:3]
-    norm_lines = norm_cols.T
-    gain1, gain2, bias1, bias2 = [norm_lines[k][None, :] for k in range(4)]
-    out_full = gather_fsdp(w_out)
-    up_half = jnp.concatenate([w_up, swap_x(w_up)], axis=1)
-    down_half = jnp.concatenate([w_down, swap_x(w_down)], axis=0)
-    fresh_width = VH * HD
+        first_parts.append(
+            lax.ppermute(jnp.where((ctx + s) % 4 == 1, message[0], message[1]), "ctx", pairs)
+        )
+
+    norms = jnp.pad(jnp.concatenate([norm_gains, norm_biases], axis=0), ((0, 12), (0, D - D // 4)))
+    out_norms = jnp.concatenate([w_out, norms], axis=0)
+    out_other = swap_x(out_norms)
+    cot_own = cotangent[0]
+    cot_far = swap_core(cot_own)
+
+    ring_a.append(shift_ctx(ring_a[1], 1))
+    ring_b.append(shift_ctx(ring_b[1], 1))
+    qkv_pair = swap_core(after(jnp.stack([w_qkv, qkv_other]), ring_a[1], ring_b[1]))
+    out_pair = swap_core(jnp.stack([out_norms, out_other]))
+    down_other = swap_x(after(w_down, qkv_other))
+    up_other = swap_x(after(w_up, qkv_other))
+    qkv_full = jnp.concatenate(in_fsdp_order(fsdp, w_qkv, qkv_other, qkv_pair), axis=0)
+    out_parts = in_fsdp_order(fsdp, out_norms, out_other, out_pair)
+    out_full = jnp.concatenate([part[: D // 4] for part in out_parts], axis=0)
+    lines = jnp.concatenate(
+        [part[D // 4 : D // 4 + 4, : D // 4] for part in out_parts], axis=1
+    ).astype(jnp.float32)
     grouped = []
     for g in range(4):
         wv = (
             qkv_full[:, 2 * D + g * GW : 2 * D + (g + 1) * GW]
-            if (g + 1) * GW <= fresh_width
+            if (g + 1) * GW <= VH * HD
             else jnp.zeros((D, GW), jnp.bfloat16)
         )
         grouped.append(
@@ -583,113 +887,68 @@
             )
         )
     grouped = jnp.stack(grouped)
-    w_groups = [lax.dynamic_index_in_dim(grouped, group_at[s], 0, keepdims=False) for s in range(4)]
-    w_own = w_groups[0]
-    w_turned = jnp.concatenate(w_groups, axis=1)
-    out_turned = jnp.concatenate(
-        [lax.dynamic_slice_in_dim(out_full, group_at[s] * GW, GW, axis=0) for s in range(4)], axis=0
-    )
-
-    chunk = layer_input[0]
-    half = rows // 2
-    parts = [chunk[:half], chunk[half:]]
-    slots = [chunk]
-    for s in range(3):
-        parts = [shift_ctx(part, 1) for part in parts]
-        slots.append(jnp.concatenate(parts, axis=0))
-    unit_slots, qkv_slots = [], []
+    ring_a.append(shift_ctx(ring_a[2], 1))
+    ring_b.append(shift_ctx(ring_b[2], 1))
+
+    held = None
     for s in range(4):
-        unit, spread = normalize(slots[s].astype(jnp.float32))
-        if s == 0:
-            own_unit, own_spread = unit, spread
-        h_one = (unit * gain1 + bias1).astype(jnp.bfloat16)
-        part = dot32(h_one, w_own).astype(jnp.bfloat16)
-        value = jnp.where(reuses, first_parts[s], part[:, 2 * GW :])
-        qkv_slots.append(jnp.concatenate([part[:, : 2 * GW], value], axis=1))
-        unit_slots.append(unit.astype(jnp.bfloat16))
-    qkv_heads = jnp.concatenate(qkv_slots, axis=0)
-    unit_all = jnp.concatenate(unit_slots, axis=0)
-
-    cot_own = cotangent[0]
-    cot_both = jnp.concatenate([cot_own, swap_core(cot_own)], axis=0)
-    dactive = dot_nt(cot_both, down_half).astype(jnp.bfloat16)
-
-    mixed, mixed_t, lse = attn_forward(roff, jmin, starts, qkv_heads)
-    pieces = [mixed[:rows]] + [
-        shift_ctx(mixed[s * rows : (s + 1) * rows], -s) for s in range(1, 4)
-    ]
-    attn_low = jnp.concatenate(pieces, axis=1)
-    resid = chunk.astype(jnp.float32) + dot32(attn_low, out_turned)
-    unit_two, spread_two = normalize(resid)
-    h_two = (unit_two * gain2 + bias2).astype(jnp.bfloat16)
-    h_both = jnp.concatenate([h_two, swap_core(h_two)], axis=0)
-
-    upper = dot32(h_both, up_half)
-    root = 0.7978845608028654
-    squared = upper * upper
-    tanned = jnp.tanh(root * upper * (1.0 + 0.044715 * squared))
-    active_low = (0.5 * upper * (1.0 + tanned)).astype(jnp.bfloat16)
-    slope = 0.5 * (1.0 + tanned) + 0.5 * upper * (1.0 - tanned * tanned) * root * (
-        1.0 + 3.0 * 0.044715 * squared
-    )
-    dupper_low = (dactive.astype(jnp.float32) * slope).astype(jnp.bfloat16)
-
-    dh_both = dot_nt(dupper_low, up_half)
-    dh_two = dh_both[:rows] + swap_core(dh_both[rows:].astype(jnp.bfloat16)).astype(jnp.float32)
-    gain_two_grad = jnp.sum(dh_two * unit_two, axis=0)
-    bias_two_grad = jnp.sum(dh_two, axis=0)
-    dresid = cot_own.astype(jnp.float32) + norm_back(dh_two, unit_two, spread_two, gain2)
-    dbranch_low = dresid.astype(jnp.bfloat16)
-    dmixed = dot_nt(dbranch_low, out_turned).astype(jnp.bfloat16)
-    dmixed_slots = [dmixed[:, :GW]] + [
-        shift_ctx(dmixed[:, s * GW : (s + 1) * GW], s) for s in range(1, 4)
-    ]
-    dmixed_all = jnp.concatenate(dmixed_slots, axis=0)
-
-    out_both = dot32(active_low, down_half)
+        held = project(s, ids, ring_a[s], ring_b[s], grouped, lines, first_parts[s], held)
+    unit_t, qkv_heads = held
+
+    forward = attn_forward(roff, jmin, starts, qkv_heads)
+    mixed, mixed_t, lse = forward[:4], forward[4], forward[5]
+    pieces = [mixed[0]] + [shift_ctx(mixed[s], -s) for s in range(1, 4)]
+    cot_both = after(jnp.concatenate([cot_own, cot_far], axis=0), mixed[0])
+    dactive = jnp.concatenate([dot_nt(cot_both, w_down), dot_nt(cot_both, down_other)], axis=1).astype(
+        jnp.bfloat16
+    )
+    resid, h_two, attn_low = residual(groups, chunk, pieces, out_full, lines)
+    h_far = swap_core(h_two)
+    g_mine, g_other, du_mine, du_other, dh_own, dh_far = feed(h_two, h_far, dactive, w_up, up_other)
+    dh_back = swap_core(dh_far)
+    dresid, dbranch_low, d0, d1, d2, d3, sums2 = branch(
+        groups, dh_own, dh_back, resid, cot_own, lines, out_full
+    )
+    dmixed = [d0] + [shift_ctx(d, s) for s, d in ((1, d1), (2, d2), (3, d3))]
+
+    g_other, du_other, g_mine, du_mine = lax.optimization_barrier(
+        (g_other, du_other, g_mine, du_mine, d1)
+    )[:4]
+    h_both = jnp.concatenate([h_two, h_far], axis=0)
+    down_far = swap_x(dot_tn(g_other, cot_both).astype(jnp.bfloat16))
+    up_far = swap_x(dot_tn(h_both, du_other).astype(jnp.bfloat16))
+    out_turned_grad = dot_tn(attn_low, dbranch_low)
+    out_shares = out_turned_grad.reshape(4, GW, D)
+    out_sum = reduce_fsdp(
+        jnp.stack(
+            [lax.dynamic_index_in_dim(out_shares, place[g], 0, keepdims=False) for g in range(4)]
+        ),
+        fsdp,
+    )
+    down_mine = dot_tn(g_mine, cot_both)
+    up_mine = dot_tn(h_both, du_mine)
+    down_sum = down_mine + down_far.astype(jnp.float32)
+    up_sum = up_mine + up_far.astype(jnp.float32)
+    down_low, up_low, out_low = lax.psum(
+        (down_sum.astype(jnp.bfloat16), up_sum.astype(jnp.bfloat16), out_sum.astype(jnp.bfloat16)),
+        ("dp", "ctx"),
+    )
+    out_both = dot32(g_mine, w_down) + dot32(g_other, down_other)
     layer_out = (
         resid + out_both[:rows] + swap_core(out_both[rows:].astype(jnp.bfloat16)).astype(jnp.float32)
     ).astype(jnp.bfloat16)
 
-    down_grad = dot_tn(active_low, cot_both)
-    up_grad = dot_tn(h_both, dupper_low)
-    width = w_up.shape[1]
-    down_sum = down_grad[:width] + swap_x(down_grad[width:].astype(jnp.bfloat16)).astype(jnp.float32)
-    up_sum = up_grad[:, :width] + swap_x(up_grad[:, width:].astype(jnp.bfloat16)).astype(jnp.float32)
-    out_turned_grad = dot_tn(attn_low, dbranch_low)
-    out_parts = out_turned_grad.reshape(4, GW, D)
-    place = jnp.array([GROUP_OF.index(g) for g in range(4)], jnp.int32)
-    out_rows = [
-        lax.dynamic_index_in_dim(out_parts, (place[g] - ctx) % 4, 0, keepdims=False) for g in range(4)
-    ]
-    shares = jnp.stack(out_rows)
-    out_sum = reduce_fsdp(shares, fsdp)
-    down_low, up_low, out_low = lax.psum(
-        (down_sum.astype(jnp.bfloat16), up_sum.astype(jnp.bfloat16), out_sum.astype(jnp.bfloat16)),
-        ("dp", "ctx"),
-    )
-
-    dqkv = attn_backward(roff, jmin, starts, qkv_heads, dmixed_all, mixed_t, lse)
-    back = [dqkv[:rows]] + [shift_ctx(dqkv[s * rows : (s + 1) * rows], -s) for s in range(1, 4)]
-
-    product = dot_tn(unit_all, dqkv)
-    sums = jnp.sum(dqkv.astype(jnp.float32), axis=0, keepdims=True)
-    w_own32 = w_own.astype(jnp.float32)
-    gain_one_col = jnp.sum(w_own32 * product, axis=1, keepdims=True)
-    bias_one_col = jnp.sum(w_own32 * sums, axis=1, keepdims=True)
-    qkv_part = gain1_col * product + bias1_col * sums
-    extra = jnp.concatenate(
-        [gain_one_col, gain_two_grad[:, None], bias_one_col, bias_two_grad[:, None], jnp.zeros((D, 60), jnp.float32)],
-        axis=1,
-    )
-    share = jnp.concatenate([qkv_part, extra], axis=1).reshape(4, D // 4, 3 * GW + 64)
+    backward = attn_backward(roff, jmin, starts, qkv_heads, dmixed, mixed_t, lse)
+    dqkv = backward[0]
+    back = [backward[1]] + [shift_ctx(backward[1 + s], -s) for s in range(1, 4)]
+
+    share = qkv_product(ids, unit_t, dqkv, grouped, lines, sums2).reshape(4, D // 4, 3 * GW + 64)
     share = reduce_fsdp(share, fsdp)
     share_low = share.astype(jnp.bfloat16)
-    share = share + swap_dp(share_low).astype(jnp.float32)
-    share_low = share.astype(jnp.bfloat16)
+    share_low = (share + swap_dp(share_low).astype(jnp.float32)).astype(jnp.bfloat16)
     others = jnp.stack([share_low] + [shift_ctx(share_low, -s) for s in range(1, 4)])
     by_group = [
-        lax.dynamic_index_in_dim(others, (place[g] - ctx) % 4, 0, keepdims=False).astype(jnp.float32)
+        lax.dynamic_index_in_dim(others, place[g], 0, keepdims=False).astype(jnp.float32)
         for g in range(4)
     ]
     qkv_grad = jnp.concatenate(
@@ -698,21 +957,10 @@
         + [by_group[g][:, 2 * GW : 3 * GW] for g in range(2)],
         axis=1,
     )
-    tails = sum(b[:, 3 * GW : 3 * GW + 4] for b in by_group)
-    norm_grads = tails.T
+    norm_grads = sum(b[:, 3 * GW : 3 * GW + 4] for b in by_group).T
     gains_grad, biases_grad = norm_grads[:2], norm_grads[2:4]
 
-    back_all = jnp.concatenate(back, axis=1)
-    dh_one = dot_nt(back_all, w_turned)
-    input_grad = dresid + norm_back(dh_one, own_unit, own_spread, gain1)
-    value_parts = jnp.stack([b[:, 2 * GW :] for b in back])
-    first_grad = jnp.concatenate(
-        [
-            lax.dynamic_index_in_dim(value_parts, (place[g] - ctx) % 4, 0, keepdims=False)
-            for g in (2, 3)
-        ],
-        axis=1,
-    ).astype(jnp.float32)
+    input_grad, first_grad = input_gradient(groups, place, chunk, dresid, back, grouped, lines)
 
     return (
         layer_out[None],

time: 557 us -> 459 us (0.82)
  local copies, waits for them, and re-layouts: 76.3 us -> 18.9 us
  waiting for transfers between devices: 228 us -> 175 us
  Pallas kernels: 54.1 us -> 107 us
  matrix products: 47.5 us -> 27.2 us
  other arithmetic: 61.5 us -> 41.5 us
    pallas_call x2 -> x11, Pallas kernels: 54.1 us -> 107 us  [the longest x1 25.2 us: attn_backward(): pl.pallas_call(attn_bwd_kernel, name='attn_backward', out_shape=(jax.Shap...]
    psum x1, waiting for transfers between devices: 81.3 us -> 48.4 us  [grouped_body(): lax.psum((down_sum.astype(jnp.bfloat16), up_sum.astype(jnp.bfloat16), out...]
    concatenate x8 -> x1, local copies, waits for them, and re-layouts: 16.3 us -> 0.05 us  [grouped_body(): h_both = jnp.concatenate([h_two, h_far], axis=0)]
    slice x18 -> x8, local copies, waits for them, and re-layouts: 18.2 us -> 2.02 us  [the longest x1 1.17 us: grouped_body(): xa, xb = (chunk[:BLK], chunk[BLK:])]
    convert_element_type x10 -> x3, other arithmetic: 14 us -> 1.84 us  [the longest x1 1.02 us: grouped_body(): (share + swap_dp(share_low).astype(jnp.float32)).astype(jnp.bfloat16)]
    dot_general x4 -> x2, matrix products: 17.5 us -> 5.37 us  [dot_nt(): lax.dot_general(a, b, (((1,), (1,)), ((), ())), preferred_element_type=jn...]
    dynamic_slice x9 -> x1, local copies, waits for them, and re-layouts: 11.5 us -> 0.16 us  [grouped_body(): lax.dynamic_index_in_dim(out_shares, place[g], 0, keepdims=False)]
    ppermute x1, waiting for transfers between devices: 10.3 us -> 0.01 us  [swap_dp(): return lax.ppermute(value, 'dp', [(0, 1), (1, 0)])]
  transfers between devices with their start and end apart: 39 -> 39, of which waited for: 18 -> 12; matrix products, arithmetic and copies ran while one was open for 30% -> 16% of each run, Pallas kernels for 10% -> 19%
where the time goes in v2:
time: 459 us; the launch traced here: 453 us
  waiting for transfers between devices  175 us (38%)
  Pallas kernels  107 us (23%)
  starting transfers between devices  60.4 us (13%)
  other arithmetic  41.5 us (9%)
  matrix products  27.2 us (6%)
  between operations  22.4 us (5%)
  local copies, waits for them, and re-layouts  18.9 us (4%)
    ppermute x18, waiting for transfers between devices, shift_ctx(): return lax.ppermute(value, 'ctx', [(i, (i + shift) % 4) for i in range(4)])  108 us
    psum x1, waiting for transfers between devices, grouped_body(): lax.psum((down_sum.astype(jnp.bfloat16), up_sum.astype(jnp.bfloat16), out...  48.4 us
    ppermute x18, starting transfers between devices, shift_ctx(): return lax.ppermute(value, 'ctx', [(i, (i + shift) % 4) for i in range(4)])  32.4 us
    pallas_call x1, Pallas kernels, attn_backward(): pl.pallas_call(attn_bwd_kernel, name='attn_backward', out_shape=(jax.Shap...  25.2 us
    pallas_call x1, Pallas kernels, attn_forward(): pl.pallas_call(attn_fwd_kernel, name='attn_forward', out_shape=(*[jax.Sha...  22.8 us
    ppermute x8, waiting for transfers between devices, swap_x(): return lax.ppermute(value, 'fsdp', [(i, i ^ 2) for i in range(4)])  19.1 us
    pallas_call x4, Pallas kernels, project(): pl.pallas_call(project_kernel, name='project_' + str(slot), grid_spec=plt...  18.3 us
    ppermute x8, starting transfers between devices, swap_x(): return lax.ppermute(value, 'fsdp', [(i, i ^ 2) for i in range(4)])  14.4 us
  transfers between devices with their start and end apart: 39, of which 12 were waited for; matrix products, arithmetic and copies ran while one was open for 16% of the time, Pallas kernels for 19%

profile of v2, /device:TPU:0, one launch (start us, length us, event | category | flops | bytes accessed | tf_op | source)
XLA Modules:
  0.0 452.5 jit_solution(5759209558277011329)
XLA Ops:
  19.5 4.3 collective-permute-start.12
  25.6 10.6 %collective-permute-done.6 = bf16[192,1920]{1,0:T(8,128)(2,1)S(1)} collective-permute-done((bf16[192,1920]{1,0:T(8,128)(2,1)}, bf16[192,1920]{1,0:T(8,128)(2,1)S(1)}, u32[]{:S(2)}, u32[]{:S(2)}) %collective-permute-start.6) | collective-permute-done | bytes 737312 | tf_op jit(solution)/shard_map/ppermute | solution.py:766
  36.2 5.4 %collective-permute-start.11 = (bf16[256,384]{1,0:T(8,128)(2,1)}, bf16[256,384]{1,0:T(8,128)(2,1)}, u32[]{:S(2)}, u32[]{:S(2)}) collective-permute-start(bf16[256,384]{1,0:T(8,128)(2,1)} %get-tuple-element.162), channel_id=1, source_target_pairs={{0,8},{12,4},{1,9},{13,5},{2,10},{14,6},{3,11},{15,7},{16,24},{28,... | collective-permute-start | bytes 589832 | tf_op jit(solution)/shard_map/ppermute | solution.py:855
  53.8 9.7 %collective-permute-done.1.xa = bf16[256,768]{1,0:T(8,128)(2,1)} collective-permute-done((bf16[256,768]{1,0:T(8,128)(2,1)}, bf16[256,768]{1,0:T(8,128)(2,1)}, u32[]{:S(2)}, u32[]{:S(2)}) %collective-permute-start.1) | collective-permute-done | bytes 393248 | tf_op jit(solution)/shard_map/ppermute | solution.py:758
  64.9 6.5 %collective-permute-done.4.xb = bf16[256,768]{1,0:T(8,128)(2,1)} collective-permute-done((bf16[256,768]{1,0:T(8,128)(2,1)}, bf16[256,768]{1,0:T(8,128)(2,1)}, u32[]{:S(2)}, u32[]{:S(2)}) %collective-permute-start.4) | collective-permute-done | bytes 393248 | tf_op jit(solution)/shard_map/ppermute | solution.py:758
  73.4 4.5 %pad_maximum_fusion.3 = bf16[768,1920]{1,0:T(8,128)(2,1)S(1)} fusion(bf16[192,1920]{1,0:T(8,128)(2,1)S(1)} %get-tuple-element.140, bf16[192,1920]{1,0:T(8,128)(2,1)S(1)} %get-tuple-element.141, bf16[192,1920]{1,0:T(8,128)(2,1)S(1)} %get-tuple-element.142, bf16[192,1920]{1,0:T(8,128)(2,1)S(1)} %get-tuple-element.139), kind=kLoop, calls=%fused_computation.4 | loop fusion | flops 11796480 | bytes 5898240 | tf_op jit(solution)/shard_map/concatenate | solution.py:870
  83.8 4.5 %project_0.1 = (bf16[768,2048]{1,0:T(8,128)(2,1)}, bf16[2048,576]{1,0:T(8,128)(2,1)}) custom-call(s32[2]{0:T(128)} %pad_add_fusion.ids, bf16[256,768]{1,0:T(8,128)(2,1)} %copy-done.14, bf16[256,768]{1,0:T(8,128)(2,1)} %copy-done.13, bf16[4,768,576]{2,1,0:T(8,128)(2,1)} %pad_maximum_fusion.w_ref, f32[4,768]{1,0:T(4,128)} %maximum_convert_fusion.lines, ...), custom_call_target="tpu_custom_call" | custom-call | tf_op jit(solution)/shard_map/project_0/pallas_call | solution.py:516
  88.3 4.6 %project_1.1 = (bf16[768,2048]{1,0:T(8,128)(2,1)}, bf16[2048,576]{1,0:T(8,128)(2,1)}) custom-call(s32[2]{0:T(128)} %pad_add_fusion.ids, bf16[256,768]{1,0:T(8,128)(2,1)} %collective-permute-done.xa, bf16[256,768]{1,0:T(8,128)(2,1)} %collective-permute-done.3.xb, ...), custom_call_target="tpu_custom_call", output_to_operand_aliasing={{0}: (6, {}), {1}: (7, {})} | custom-call | tf_op jit(solution)/shard_map/project_1/pallas_call | solution.py:516
  94.4 4.6 %project_2.1 = (bf16[768,2048]{1,0:T(8,128)(2,1)}, bf16[2048,576]{1,0:T(8,128)(2,1)}) custom-call(s32[2]{0:T(128)} %pad_add_fusion.ids, bf16[256,768]{1,0:T(8,128)(2,1)} %collective-permute-done.1.xa, bf16[256,768]{1,0:T(8,128)(2,1)} %collective-permute-done.4.xb, ...), custom_call_target="tpu_custom_call", output_to_operand_aliasing={{0}: (6, {}), {1}: (7, {})} | custom-call | tf_op jit(solution)/shard_map/project_2/pallas_call | solution.py:516
  99.9 4.6 %project_3.1 = (bf16[768,2048]{1,0:T(8,128)(2,1)}, bf16[2048,576]{1,0:T(8,128)(2,1)}) custom-call(s32[2]{0:T(128)} %pad_add_fusion.ids, bf16[256,768]{1,0:T(8,128)(2,1)} %copy-done.25, bf16[256,768]{1,0:T(8,128)(2,1)} %copy-done.26, bf16[4,768,576]{2,1,0:T(8,128)(2,1)} %pad_maximum_fusion.w_ref, ...), custom_call_target="tpu_custom_call", output_to_operand_aliasing={{0}: (6, {}), {1}: (7, {})} | custom-call | tf_op jit(solution)/shard_map/project_3/pallas_call | solution.py:516
  104.5 22.8 %attn_forward.1 = (bf16[256,384]{1,0:T(8,128)(2,1)}, bf16[256,384]{1,0:T(8,128)(2,1)}, bf16[256,384]{1,0:T(8,128)(2,1)}, bf16[256,384]{1,0:T(8,128)(2,1)}, f32[3...) custom-call(s32[8]{0:T(128)} %fusion.22.roff, s32[8]{0:T(128)} %convert_reduce_fusion.1.jmin, s32[8,256]{1,0:T(8,128)} %reshape.49.start_ref, ...), custom_call_target="tpu_custom_call" | custom-call | tf_op jit(solution)/shard_map/attn_forward/pallas_call | solution.py:428
  127.4 7.1 %collective-permute-start.13 = (bf16[256,384]{1,0:T(8,128)(2,1)}, bf16[256,384]{1,0:T(8,128)(2,1)S(1)}, u32[]{:S(2)}, u32[]{:S(2)}) collective-permute-start(bf16[256,384]{1,0:T(8,128)(2,1)} %get-tuple-element.63), channel_id=1, source_target_pairs={{0,12},{4,0},{8,4},{12,8},{1,13},{5,1},{9,5},{13,9},{2,14},{6,2},{... | collective-permute-start | bytes 589832 | tf_op jit(solution)/shard_map/ppermute | solution.py:758
  138.6 12.4 %collective-permute-done.14.m2 = bf16[256,384]{1,0:T(8,128)(2,1)S(1)} collective-permute-done((bf16[256,384]{1,0:T(8,128)(2,1)}, bf16[256,384]{1,0:T(8,128)(2,1)S(1)}, u32[]{:S(2)}, u32[]{:S(2)}) %collective-permute-start.14) | collective-permute-done | bytes 196640 | tf_op jit(solution)/shard_map/ppermute | solution.py:758
  151.8 4.5 residual.1
  164.9 13.6 %feed.1 = (bf16[1024,768]{1,0:T(8,128)(2,1)}, bf16[1024,768]{1,0:T(8,128)(2,1)}, bf16[1024,768]{1,0:T(8,128)(2,1)}, bf16[1024,768]{1,0:T(8,128)(2,1)}, f32[512,768]{1,0:T(8,128)}, /*index=5*/bf16[512,768]{1,0:T(8,128)(2,1)}) custom-call(bf16[512,768]{1,0:T(8,128)(2,1)} %get-tuple-element.67.ha, bf16[512,768]{1,0:T(8,128)(2,1)} %copy-done.3, ...), custom_call_target="tpu_custom_call" | custom-call | tf_op jit(solution)/shard_map/feed/pallas_call | solution.py:620
  188.3 6.0 %branch.1 = (f32[512,768]{1,0:T(8,128)}, bf16[512,768]{1,0:T(8,128)(2,1)}, bf16[256,384]{1,0:T(8,128)(2,1)}, bf16[256,384]{1,0:T(8,128)(2,1)}, bf16[256,384]{1,0...) custom-call(s32[4]{0:T(128)} %copy-done.39, f32[512,768]{1,0:T(8,128)} %get-tuple-element.75.dh_ref, ...), custom_call_target="tpu_custom_call" | custom-call | tf_op jit(solution)/shard_map/branch/pallas_call | solution.py:665
  198.6 3.3 collective-permute-start.37
  209.3 4.4 fusion.36
  218.8 25.2 %attn_backward.1 = (bf16[2048,576]{1,0:T(8,128)(2,1)}, bf16[256,1152]{1,0:T(8,128)(2,1)}, bf16[256,1152]{1,0:T(8,128)(2,1)}, bf16[256,1152]{1,0:T(8,128)(2,1)}, bf16[256,1152]{1,0:T(8,128)(2,1)}) custom-call(s32[8]{0:T(128)} %fusion.22.roff, s32[8]{0:T(128)} %convert_reduce_fusion.1.jmin, s32[8,256]{1,0:T(8,128)} %reshape.49.start_ref, ...), custom_call_target="tpu_custom_call" | custom-call | tf_op jit(solution)/shard_map/attn_backward/pallas_call | solution.py:451
  243.9 8.1 %qkv_product.1 = f32[768,640]{1,0:T(8,128)} custom-call(s32[2]{0:T(128)} %pad_add_fusion.ids, bf16[768,2048]{1,0:T(8,128)(2,1)} %get-tuple-element.92.unit_ref, bf16[2048,576]{1,0:T(8,128)(2,1)} %get-tuple-element.93.dqkv_ref, bf16[4,768,576]{2,1,0:T(8,128)(2,1)} %pad_maximum_fusion.w_ref, f32[4,768]{1,0:T(4,128)} %maximum_convert_fusion.lines, ...), custom_call_target="tpu_custom_call" | custom-call | tf_op jit(solution)/shard_map/qkv_product/pallas_call | solution.py:700
  255.0 4.1 convolution_add_fusion
  261.3 6.8 %collective-permute-start.25 = (bf16[256,1152]{1,0:T(8,128)(2,1)}, bf16[256,1152]{1,0:T(8,128)(2,1)S(1)}, u32[]{:S(2)}, u32[]{:S(2)}) collective-permute-start(bf16[256,1152]{1,0:T(8,128)(2,1)} %get-tuple-element.87), channel_id=1, source_target_pairs={{0,12},{4,0},{8,4},{12,8},{1,13},{5,1},{9,5},{13,9},{2,14},{6,2},{... | collective-permute-start | bytes 1769480 | tf_op jit(solution)/shard_map/ppermute | solution.py:758
  269.4 3.3 collective-permute-start.35
  272.9 7.0 %collective-permute-done.35 = bf16[192,768]{1,0:T(8,128)(2,1)S(1)} collective-permute-done((bf16[192,768]{1,0:T(8,128)(2,1)S(1)}, bf16[192,768]{1,0:T(8,128)(2,1)S(1)}, u32[]{:S(2)}, u32[]{:S(2)}) %collective-permute-start.35) | collective-permute-done | bytes 294944 | tf_op jit(solution)/shard_map/ppermute | solution.py:766
  281.8 3.8 add_convert_fusion
  287.3 3.7 add_convert_fusion.1
  293.4 54.0 %collective-permute-done.26.b2 = bf16[256,1152]{1,0:T(8,128)(2,1)S(1)} collective-permute-done((bf16[256,1152]{1,0:T(8,128)(2,1)}, bf16[256,1152]{1,0:T(8,128)(2,1)S(1)}, u32[]{:S(2)}, u32[]{:S(2)}) %collective-permute-start.26) | collective-permute-done | bytes 589856 | tf_op jit(solution)/shard_map/ppermute | solution.py:758
  348.4 8.3 %input_gradient.1 = (f32[512,768]{1,0:T(8,128)}, f32[512,384]{1,0:T(8,128)}) custom-call(s32[4]{0:T(128)} %copy-done.39, s32[4]{0:T(128)} %copy-done.38, bf16[512,768]{1,0:T(8,128)(2,1)} %bitcast.124, f32[512,768]{1,0:T(8,128)} %get-tuple-element.80.dresid_ref, bf16[256,1152]{1,0:T(8,128)(2,1)} %get-tuple-element.86.b0, bf16[256,1152]{1,0:T(8,128)(2,1)} %copy-done.21, ...), custom_call_target="tpu_custom_call" | custom-call | tf_op jit(solution)/shard_map/input_gradient/pallas_call | solution.py:741
  357.8 3.8 collective-permute-start.32
  366.4 4.2 collective-permute-done.31
  370.6 17.2 %collective-permute-done.32 = bf16[192,640]{1,0:T(8,128)(2,1)S(1)} collective-permute-done((bf16[192,640]{1,0:T(8,128)(2,1)S(1)}, bf16[192,640]{1,0:T(8,128)(2,1)S(1)}, u32[]{:S(2)}, u32[]{:S(2)}) %collective-permute-start.32) | collective-permute-done | bytes 245792 | tf_op jit(solution)/shard_map/ppermute | solution.py:758
  391.6 48.4 %all-reduce.4.cloned.1.call-done = (bf16[192,768]{1,0:T(8,128)(2,1)}, bf16[768,768]{1,0:T(8,128)(2,1)}, bf16[768,768]{1,0:T(8,128)(2,1)}) async-done(((bf16[192,768]{1,0:T(8,128)(2,1)}, bf16[768,768]{1,0:T(8,128)(2,1)}, bf16[768,768]{1,0:T(8,128)(2,1)}), (bf16[192,768]{1,0:T(8,128)(2,1)}, bf16[768,768]{1,0:T(8,128)(2,1)}, bf16[768,768]{1,0:T(8,128)(2,1)})) %all-reduce.4.cloned.1.call-update) | async-done | bytes 2654224 | tf_op jit(solution)/shard_map/psum | solution.py:932
  (233 shorter events, 98.7 us)
Async XLA Ops:
  7.2 432.9 %all-reduce.4.cloned.1.call-start = ((), (), s32[]{:S(2)}) async-start(), calls=%async_computation | async-start | bytes 5308416 | tf_op jit(solution)/shard_map/psum | solution.py:932
  9.7 33.9 %collective-permute-start.8 = (bf16[208,768]{1,0:T(8,128)(2,1)}, bf16[208,768]{1,0:T(8,128)(2,1)}, u32[]{:S(2)}, u32[]{:S(2)}) collective-permute-start(bf16[208,768]{1,0:T(8,128)(2,1)} %get-tuple-element.179), channel_id=1, source_target_pairs={{0,2},{1,3},{2,0},{3,1},{4,6},{5,7},{6,4},{7,5},{8,10},{9,11},{10,... | collective-permute-start | bytes 958472 | tf_op jit(solution)/shard_map/ppermute | solution.py:766
  12.7 23.5 %collective-permute-start.6 = (bf16[192,1920]{1,0:T(8,128)(2,1)}, bf16[192,1920]{1,0:T(8,128)(2,1)S(1)}, u32[]{:S(2)}, u32[]{:S(2)}) collective-permute-start(bf16[192,1920]{1,0:T(8,128)(2,1)} %param.17), channel_id=1, source_target_pairs={{0,2},{1,3},{2,0},{3,1},{4,6},{5,7},{6,4},{7,5},{8,10},{9,11},{10,... | collective-permute-start | bytes 2211848 | tf_op jit(solution)/shard_map/ppermute | solution.py:766
  13.9 29.0 %collective-permute-start = (bf16[256,768]{1,0:T(8,128)(2,1)S(1)}, bf16[256,768]{1,0:T(8,128)(2,1)}, u32[]{:S(2)}, u32[]{:S(2)}) collective-permute-start(bf16[256,768]{1,0:T(8,128)(2,1)S(1)} %get-tuple-element.160.xa), channel_id=1, source_target_pairs={{0,4},{4,8},{8,12},{12,0},{1,5},{5,9},{9,13},{13,1},{2,6},{6,10},{... | collective-permute-start | bytes 1179656 | tf_op jit(solution)/shard_map/ppermute | solution.py:758
  16.0 27.0 %collective-permute-start.3 = (bf16[256,768]{1,0:T(8,128)(2,1)S(1)}, bf16[256,768]{1,0:T(8,128)(2,1)}, u32[]{:S(2)}, u32[]{:S(2)}) collective-permute-start(bf16[256,768]{1,0:T(8,128)(2,1)S(1)} %get-tuple-element.159.xb), channel_id=1, source_target_pairs={{0,4},{4,8},{8,12},{12,0},{1,5},{5,9},{9,13},{13,1},{2,6},{6,10},{... | collective-permute-start | bytes 1179656 | tf_op jit(solution)/shard_map/ppermute | solution.py:758
  19.5 61.0 %collective-permute-start.12 = (bf16[256,384]{1,0:T(8,128)(2,1)}, bf16[256,384]{1,0:T(8,128)(2,1)}, u32[]{:S(2)}, u32[]{:S(2)}) collective-permute-start(bf16[256,384]{1,0:T(8,128)(2,1)} %get-tuple-element.163), channel_id=1, source_target_pairs={{0,4},{4,8},{1,5},{5,9},{2,6},{6,10},{3,7},{7,11},{16,20},{20,24},... | collective-permute-start | bytes 589832 | tf_op jit(solution)/shard_map/ppermute | solution.py:855
  36.2 56.7 %collective-permute-start.11 = (bf16[256,384]{1,0:T(8,128)(2,1)}, bf16[256,384]{1,0:T(8,128)(2,1)}, u32[]{:S(2)}, u32[]{:S(2)}) collective-permute-start(bf16[256,384]{1,0:T(8,128)(2,1)} %get-tuple-element.162), channel_id=1, source_target_pairs={{0,8},{12,4},{1,9},{13,5},{2,10},{14,6},{3,11},{15,7},{16,24},{28,... | collective-permute-start | bytes 589832 | tf_op jit(solution)/shard_map/ppermute | solution.py:855
  43.0 28.4 %collective-permute-start.7 = (bf16[2,192,1920]{2,1,0:T(8,128)(2,1)}, bf16[2,192,1920]{2,1,0:T(8,128)(2,1)}, u32[]{:S(2)}, u32[]{:S(2)}) collective-permute-start(bf16[2,192,1920]{2,1,0:T(8,128)(2,1)} %pad_maximum_fusion.6), channel_id=1, source_target_pairs={{0,1},{1,0},{2,3},{3,2},{4,5},{5,4},{6,7},{7,6},{8,9},{9,8},{10,11... | collective-permute-start | bytes 4423688 | tf_op jit(solution)/shard_map/ppermute | solution.py:762
  49.4 14.0 %collective-permute-start.1 = (bf16[256,768]{1,0:T(8,128)(2,1)}, bf16[256,768]{1,0:T(8,128)(2,1)}, u32[]{:S(2)}, u32[]{:S(2)}) collective-permute-start(bf16[256,768]{1,0:T(8,128)(2,1)} %collective-permute-done.xa), channel_id=1, source_target_pairs={{0,4},{4,8},{8,12},{12,0},{1,5},{5,9},{9,13},{13,1},{2,6},{6,10},{... | collective-permute-start | bytes 1179656 | tf_op jit(solution)/shard_map/ppermute | solution.py:758
  51.8 19.6 %collective-permute-start.4 = (bf16[256,768]{1,0:T(8,128)(2,1)}, bf16[256,768]{1,0:T(8,128)(2,1)}, u32[]{:S(2)}, u32[]{:S(2)}) collective-permute-start(bf16[256,768]{1,0:T(8,128)(2,1)} %collective-permute-done.3.xb), channel_id=1, source_target_pairs={{0,4},{4,8},{8,12},{12,0},{1,5},{5,9},{9,13},{13,1},{2,6},{6,10},{... | collective-permute-start | bytes 1179656 | tf_op jit(solution)/shard_map/ppermute | solution.py:758
  63.4 95.9 %collective-permute-start.18 = (bf16[768,768]{1,0:T(8,128)(2,1)}, bf16[768,768]{1,0:T(8,128)(2,1)}, u32[]{:S(2)}, u32[]{:S(2)}) collective-permute-start(bf16[768,768]{1,0:T(8,128)(2,1)} %param.20), channel_id=1, source_target_pairs={{0,2},{1,3},{2,0},{3,1},{4,6},{5,7},{6,4},{7,5},{8,10},{9,11},{10,... | collective-permute-start | bytes 3538952 | tf_op jit(solution)/shard_map/ppermute | solution.py:766
  71.4 27.6 %collective-permute-start.2 = (bf16[256,768]{1,0:T(8,128)(2,1)}, bf16[256,768]{1,0:T(8,128)(2,1)S(1)}, u32[]{:S(2)}, u32[]{:S(2)}) collective-permute-start(bf16[256,768]{1,0:T(8,128)(2,1)} %collective-permute-done.1.xa), channel_id=1, source_target_pairs={{0,4},{4,8},{8,12},{12,0},{1,5},{5,9},{9,13},{13,1},{2,6},{6,10},{... | collective-permute-start | bytes 1179656 | tf_op jit(solution)/shard_map/ppermute | solution.py:758
  71.4 27.6 %collective-permute-start.5 = (bf16[256,768]{1,0:T(8,128)(2,1)}, bf16[256,768]{1,0:T(8,128)(2,1)S(1)}, u32[]{:S(2)}, u32[]{:S(2)}) collective-permute-start(bf16[256,768]{1,0:T(8,128)(2,1)} %collective-permute-done.4.xb), channel_id=1, source_target_pairs={{0,4},{4,8},{8,12},{12,0},{1,5},{5,9},{9,13},{13,1},{2,6},{6,10},{... | collective-permute-start | bytes 1179656 | tf_op jit(solution)/shard_map/ppermute | solution.py:758
  80.5 18.5 %collective-permute-start.10 = (bf16[256,384]{1,0:T(8,128)(2,1)S(1)}, bf16[256,384]{1,0:T(8,128)(2,1)S(1)}, u32[]{:S(2)}, u32[]{:S(2)}) collective-permute-start(bf16[256,384]{1,0:T(8,128)(2,1)S(1)} %broadcast_select_fusion.3), channel_id=1, source_target_pairs={{8,4},{12,8},{9,5},{13,9},{10,6},{14,10},{11,7},{15,11},{24,20},{2... | collective-permute-start | bytes 589832 | tf_op jit(solution)/shard_map/ppermute | solution.py:855
  92.9 71.0 %collective-permute-start.19 = (bf16[768,768]{1,0:T(8,128)(2,1)}, bf16[768,768]{1,0:T(8,128)(2,1)}, u32[]{:S(2)}, u32[]{:S(2)}) collective-permute-start(bf16[768,768]{1,0:T(8,128)(2,1)} %um.1), channel_id=1, source_target_pairs={{0,2},{1,3},{2,0},{3,1},{4,6},{5,7},{6,4},{7,5},{8,10},{9,11},{10,... | collective-permute-start | bytes 3538952 | tf_op jit(solution)/shard_map/ppermute | solution.py:766
  134.4 16.6 %collective-permute-start.14 = (bf16[256,384]{1,0:T(8,128)(2,1)}, bf16[256,384]{1,0:T(8,128)(2,1)S(1)}, u32[]{:S(2)}, u32[]{:S(2)}) collective-permute-start(bf16[256,384]{1,0:T(8,128)(2,1)} %get-tuple-element.64), channel_id=1, source_target_pairs={{0,8},{4,12},{8,0},{12,4},{1,9},{5,13},{9,1},{13,5},{2,10},{6,14},... | collective-permute-start | bytes 589832 | tf_op jit(solution)/shard_map/ppermute | solution.py:758
  134.4 16.6 %collective-permute-start.15 = (bf16[256,384]{1,0:T(8,128)(2,1)}, bf16[256,384]{1,0:T(8,128)(2,1)S(1)}, u32[]{:S(2)}, u32[]{:S(2)}) collective-permute-start(bf16[256,384]{1,0:T(8,128)(2,1)} %get-tuple-element.65), channel_id=1, source_target_pairs={{0,4},{4,8},{8,12},{12,0},{1,5},{5,9},{9,13},{13,1},{2,6},{6,10},{... | collective-permute-start | bytes 589832 | tf_op jit(solution)/shard_map/ppermute | solution.py:758
  194.3 20.7 %collective-permute-start.22 = (bf16[256,384]{1,0:T(8,128)(2,1)}, bf16[256,384]{1,0:T(8,128)(2,1)S(1)}, u32[]{:S(2)}, u32[]{:S(2)}) collective-permute-start(bf16[256,384]{1,0:T(8,128)(2,1)} %get-tuple-element.77), channel_id=1, source_target_pairs={{0,4},{4,8},{8,12},{12,0},{1,5},{5,9},{9,13},{13,1},{2,6},{6,10},{... | collective-permute-start | bytes 589832 | tf_op jit(solution)/shard_map/ppermute | solution.py:758
  198.6 82.0 %collective-permute-start.37 = (bf16[768,768]{1,0:T(8,128)(2,1)}, bf16[768,768]{1,0:T(8,128)(2,1)}, u32[]{:S(2)}, u32[]{:S(2)}) collective-permute-start(bf16[768,768]{1,0:T(8,128)(2,1)} %convolution_convert_fusion.2), channel_id=1, source_target_pairs={{0,2},{1,3},{2,0},{3,1},{4,6},{5,7},{6,4},{7,5},{8,10},{9,11},{10,... | collective-permute-start | bytes 3538952 | tf_op jit(solution)/shard_map/ppermute | solution.py:766
  204.4 81.2 %collective-permute-start.36 = (bf16[768,768]{1,0:T(8,128)(2,1)}, bf16[768,768]{1,0:T(8,128)(2,1)}, u32[]{:S(2)}, u32[]{:S(2)}) collective-permute-start(bf16[768,768]{1,0:T(8,128)(2,1)} %convolution_convert_fusion.3), channel_id=1, source_target_pairs={{0,2},{1,3},{2,0},{3,1},{4,6},{5,7},{6,4},{7,5},{8,10},{9,11},{10,... | collective-permute-start | bytes 3538952 | tf_op jit(solution)/shard_map/ppermute | solution.py:766
  204.4 13.0 %collective-permute-start.23 = (bf16[256,384]{1,0:T(8,128)(2,1)S(1)}, bf16[256,384]{1,0:T(8,128)(2,1)S(1)}, u32[]{:S(2)}, u32[]{:S(2)}) collective-permute-start(bf16[256,384]{1,0:T(8,128)(2,1)S(1)} %copy-done.46), channel_id=1, source_target_pairs={{0,8},{4,12},{8,0},{12,4},{1,9},{5,13},{9,1},{13,5},{2,10},{6,14},... | collective-permute-start | bytes 589832 | tf_op jit(solution)/shard_map/ppermute | solution.py:758
  206.3 11.8 %collective-permute-start.24 = (bf16[256,384]{1,0:T(8,128)(2,1)S(1)}, bf16[256,384]{1,0:T(8,128)(2,1)S(1)}, u32[]{:S(2)}, u32[]{:S(2)}) collective-permute-start(bf16[256,384]{1,0:T(8,128)(2,1)S(1)} %copy-done.45), channel_id=1, source_target_pairs={{0,12},{4,0},{8,4},{12,8},{1,13},{5,1},{9,5},{13,9},{2,14},{6,2},{... | collective-permute-start | bytes 589832 | tf_op jit(solution)/shard_map/ppermute | solution.py:758
  215.0 45.3 %collective-permute-start.34 = (bf16[2,192,768]{2,1,0:T(8,128)(2,1)S(1)}, bf16[2,192,768]{2,1,0:T(8,128)(2,1)S(1)}, u32[]{:S(2)}, u32[]{:S(2)}) collective-permute-start(bf16[2,192,768]{2,1,0:T(8,128)(2,1)S(1)} %fusion.3), channel_id=1, source_target_pairs={{0,1},{1,0},{2,3},{3,2},{4,5},{5,4},{6,7},{7,6},{8,9},{9,8},{10,11... | collective-permute-start | bytes 1769480 | tf_op jit(solution)/shard_map/ppermute | solution.py:762
  253.3 16.1 %collective-permute-start.28 = (bf16[2,192,640]{2,1,0:T(8,128)(2,1)S(1)}, bf16[2,192,640]{2,1,0:T(8,128)(2,1)S(1)}, u32[]{:S(2)}, u32[]{:S(2)}) collective-permute-start(bf16[2,192,640]{2,1,0:T(8,128)(2,1)S(1)} %fusion.5), channel_id=1, source_target_pairs={{0,1},{1,0},{2,3},{3,2},{4,5},{5,4},{6,7},{7,6},{8,9},{9,8},{10,11... | collective-permute-start | bytes 1474568 | tf_op jit(solution)/shard_map/ppermute | solution.py:762
  260.3 103.3 %collective-permute-start.21 = (bf16[512,768]{1,0:T(8,128)(2,1)}, bf16[512,768]{1,0:T(8,128)(2,1)}, u32[]{:S(2)}, u32[]{:S(2)}) collective-permute-start(bf16[512,768]{1,0:T(8,128)(2,1)} %slice.281), channel_id=1, source_target_pairs={{0,1},{1,0},{2,3},{3,2},{4,5},{5,4},{6,7},{7,6},{8,9},{9,8},{10,11... | collective-permute-start | bytes 2359304 | tf_op jit(solution)/shard_map/ppermute | solution.py:762
  261.3 32.1 %collective-permute-start.25 = (bf16[256,1152]{1,0:T(8,128)(2,1)}, bf16[256,1152]{1,0:T(8,128)(2,1)S(1)}, u32[]{:S(2)}, u32[]{:S(2)}) collective-permute-start(bf16[256,1152]{1,0:T(8,128)(2,1)} %get-tuple-element.87), channel_id=1, source_target_pairs={{0,12},{4,0},{8,4},{12,8},{1,13},{5,1},{9,5},{13,9},{2,14},{6,2},{... | collective-permute-start | bytes 1769480 | tf_op jit(solution)/shard_map/ppermute | solution.py:758
  279.8 67.5 %collective-permute-start.26 = (bf16[256,1152]{1,0:T(8,128)(2,1)}, bf16[256,1152]{1,0:T(8,128)(2,1)S(1)}, u32[]{:S(2)}, u32[]{:S(2)}) collective-permute-start(bf16[256,1152]{1,0:T(8,128)(2,1)} %get-tuple-element.88), channel_id=1, source_target_pairs={{0,8},{4,12},{8,0},{12,4},{1,9},{5,13},{9,1},{13,5},{2,10},{6,14},... | collective-permute-start | bytes 1769480 | tf_op jit(solution)/shard_map/ppermute | solution.py:758
  280.6 66.8 %collective-permute-start.27 = (bf16[256,1152]{1,0:T(8,128)(2,1)}, bf16[256,1152]{1,0:T(8,128)(2,1)S(1)}, u32[]{:S(2)}, u32[]{:S(2)}) collective-permute-start(bf16[256,1152]{1,0:T(8,128)(2,1)} %get-tuple-element.89), channel_id=1, source_target_pairs={{0,4},{4,8},{8,12},{12,0},{1,5},{5,9},{9,13},{13,1},{2,6},{6,10},{... | collective-permute-start | bytes 1769480 | tf_op jit(solution)/shard_map/ppermute | solution.py:758
  293.4 63.3 %collective-permute-start.30 = (bf16[192,640]{1,0:T(8,128)(2,1)}, bf16[192,640]{1,0:T(8,128)(2,1)}, u32[]{:S(2)}, u32[]{:S(2)}) collective-permute-start(bf16[192,640]{1,0:T(8,128)(2,1)} %fusion.6), channel_id=1, source_target_pairs={{0,16},{16,0},{1,17},{17,1},{2,18},{18,2},{3,19},{19,3},{4,20},{20... | collective-permute-start | bytes 737288 | tf_op jit(solution)/shard_map/ppermute | solution.py:770
  357.7 12.9 %collective-permute-start.31 = (bf16[192,640]{1,0:T(8,128)(2,1)S(1)}, bf16[192,640]{1,0:T(8,128)(2,1)S(1)}, u32[]{:S(2)}, u32[]{:S(2)}) collective-permute-start(bf16[192,640]{1,0:T(8,128)(2,1)S(1)} %add_convert_fusion.2), channel_id=1, source_target_pairs={{0,12},{4,0},{8,4},{12,8},{1,13},{5,1},{9,5},{13,9},{2,14},{6,2},{... | collective-permute-start | bytes 737288 | tf_op jit(solution)/shard_map/ppermute | solution.py:758
  357.8 30.0 %collective-permute-start.32 = (bf16[192,640]{1,0:T(8,128)(2,1)S(1)}, bf16[192,640]{1,0:T(8,128)(2,1)S(1)}, u32[]{:S(2)}, u32[]{:S(2)}) collective-permute-start(bf16[192,640]{1,0:T(8,128)(2,1)S(1)} %add_convert_fusion.2), channel_id=1, source_target_pairs={{0,8},{4,12},{8,0},{12,4},{1,9},{5,13},{9,1},{13,5},{2,10},{6,14},... | collective-permute-start | bytes 737288 | tf_op jit(solution)/shard_map/ppermute | solution.py:758
  361.6 26.2 %collective-permute-start.33 = (bf16[192,640]{1,0:T(8,128)(2,1)S(1)}, bf16[192,640]{1,0:T(8,128)(2,1)S(1)}, u32[]{:S(2)}, u32[]{:S(2)}) collective-permute-start(bf16[192,640]{1,0:T(8,128)(2,1)S(1)} %add_convert_fusion.2), channel_id=1, source_target_pairs={{0,4},{4,8},{8,12},{12,0},{1,5},{5,9},{9,13},{13,1},{2,6},{6,10},{... | collective-permute-start | bytes 737288 | tf_op jit(solution)/shard_map/ppermute | solution.py:758
  (56 other events, 534.8 us)
Sparse Core Ops, SparseCore 0:
  291.2 148.7 all-reduce.3
